TPU v7x, 512 devices: a whole 4x8x8 slice. The times are simulated.
512 devices in a mesh: seq: 8 (over x, z_hi), pos: 64 (over y, z_lo, core).
Axes of the slice: x: 4, y: 8, z: 8 (z_hi: 2, z_lo: 4; z = z_hi * 4 + z_lo), core: 2. Of those that a mesh axis runs over, the one named last changes fastest.
Arguments:
- skip_stream_input: bfloat16 [32, 512, 768], P('seq', 'pos'), may hold values from -6 to 6
- lateral_asking_vectors: bfloat16 [32, 512, 768], P('seq', 'pos'), may hold values from -30 to 30
- lateral_matched_vectors: bfloat16 [32, 512, 768], P('seq', 'pos'), may hold values from -6 to 6
- lateral_carried_vectors: bfloat16 [32, 512, 768], P('seq', 'pos'), may hold values from -6 to 6
- lateral_closing_linear: bfloat16 [768, 768], replicated, may hold values from -0.21875 to 0.21875
- upright_normalizer_multiplier: float32 [768], replicated, may hold values from 0.1 to 1.9
- upright_threefold_linear: bfloat16 [768, 2304], P(None, 'seq'), may hold values from -0.21875 to 0.21875
- upright_closing_linear: bfloat16 [768, 768], replicated, may hold values from -0.21875 to 0.21875
- regression_factors: float32 [12], replicated, may hold values from -768 to 768
- regression_offset: float32 [1], replicated, may hold values from -3 to 3
Outputs:
- alignment_output: bfloat16 [32, 512, 768], P('seq', 'pos')
- pairing_chances: float32 [512, 512], P('pos', 'seq')
All inputs are finite; a program needn't handle non-finite values.
Results may differ from a plain program's by a relative error of at most 0.004.
Values may be sent and summed in bfloat16 or wider, within the bound.
A program may use at most 64 MiB of HBM per device.

v0:
```python
import math

import jax
import jax.numpy as jnp
from jax import lax
from jax.sharding import PartitionSpec as P


def layer_norm(values, scaling):
    average = jnp.mean(values, axis=-1, keepdims=True)
    centered = values - average
    spread = jnp.mean(centered * centered, axis=-1, keepdims=True)
    return centered * lax.rsqrt(spread + 1e-05) * scaling


def column_attend(query_part, key_part, value_part, factor):
    scores = (
        jnp.einsum("sphd,tphd->phst", query_part, key_part, preferred_element_type=jnp.float32)
        * factor
    )
    exponent = jnp.exp(scores)
    col_weights = (exponent / jnp.sum(exponent, axis=-1, keepdims=True)).astype(jnp.bfloat16)
    return jnp.einsum(
        "phst,tphd->sphd", col_weights, value_part, preferred_element_type=jnp.float32
    ).astype(jnp.bfloat16)


def per_device(
    skip_stream_input,
    lateral_asking_vectors,
    lateral_matched_vectors,
    lateral_carried_vectors,
    lateral_closing_linear,
    upright_normalizer_multiplier,
    upright_threefold_linear,
    upright_closing_linear,
    regression_factors,
    regression_offset,
):
    upper_limit = lax.Precision.HIGHEST
    local_homolog_number, local_site_number, embedding_breadth = lateral_asking_vectors.shape
    focus_group_tally = regression_factors.shape[0]
    head_size = embedding_breadth // focus_group_tally
    seq_count = lax.axis_size("seq")
    pos_count = lax.axis_size("pos")
    total_len = local_site_number * pos_count
    queries = lateral_asking_vectors.reshape(
        local_homolog_number, local_site_number, focus_group_tally, head_size
    )
    shard_rows = lax.all_gather(lateral_matched_vectors, "pos", axis=1, tiled=True)
    key_part = shard_rows.reshape(
        local_homolog_number, shard_rows.shape[1], focus_group_tally, head_size
    )
    partial_value = jnp.einsum(
        "rihd,rjhd->hij", queries, key_part, preferred_element_type=jnp.float32
    )
    factor = 1.0 / (math.sqrt(head_size) * math.sqrt(local_homolog_number * seq_count))
    logits = lax.psum(partial_value, "seq") * factor
    row_peak = jnp.max(logits, axis=2, keepdims=True)
    exponent = jnp.exp(logits - row_peak)
    affinity_shares = (exponent / jnp.sum(exponent, axis=2, keepdims=True)).astype(jnp.bfloat16)
    shard_rows = lax.all_gather(lateral_carried_vectors, "pos", axis=1, tiled=True)
    row_count = shard_rows.shape[1]
    value_part = shard_rows.reshape(local_homolog_number, row_count, focus_group_tally, head_size)
    mixture = jnp.einsum(
        "hij,rjhd->rihd", affinity_shares, value_part, preferred_element_type=jnp.float32
    )
    horizontal_mixed_result = mixture.astype(jnp.bfloat16).reshape(
        local_homolog_number * local_site_number, embedding_breadth
    )
    residue_embedding = skip_stream_input.reshape(
        local_homolog_number * local_site_number, embedding_breadth
    ).astype(jnp.float32) + jnp.dot(
        horizontal_mixed_result, lateral_closing_linear, preferred_element_type=jnp.float32
    )
    normed = layer_norm(residue_embedding, upright_normalizer_multiplier).astype(jnp.bfloat16)
    full_projection = lax.all_gather(upright_threefold_linear, "seq", axis=1, tiled=True)
    col_factor = 1.0 / math.sqrt(head_size)
    all_seqs = local_homolog_number * seq_count
    grouped = lax.all_to_all(
        normed.reshape(local_homolog_number, local_site_number, embedding_breadth),
        "seq",
        split_axis=1,
        concat_axis=0,
        tiled=True,
    )
    few_pos = grouped.shape[1]
    projected = jnp.dot(
        grouped.reshape(all_seqs * few_pos, embedding_breadth),
        full_projection,
        preferred_element_type=jnp.float32,
    ).astype(jnp.bfloat16)
    projected = projected.reshape(all_seqs, few_pos, 3, focus_group_tally, head_size)
    attended = column_attend(projected[:, :, 0], projected[:, :, 1], projected[:, :, 2], col_factor)
    attended = attended.reshape(all_seqs, few_pos, embedding_breadth)
    column_mixing = lax.all_to_all(
        attended, "seq", split_axis=0, concat_axis=1, tiled=True
    ).reshape(local_homolog_number * local_site_number, embedding_breadth)
    alignment_output = (
        residue_embedding
        + jnp.dot(column_mixing, upright_closing_linear, preferred_element_type=jnp.float32)
    ).astype(jnp.bfloat16)
    alignment_output = alignment_output.reshape(
        local_homolog_number, local_site_number, embedding_breadth
    )
    pos_index = lax.axis_index("pos")
    seq_index = lax.axis_index("seq")
    row_begin = pos_index * local_site_number
    col_part = jnp.sum(affinity_shares, axis=1, dtype=jnp.float32)
    row_part = jnp.sum(affinity_shares, axis=2, dtype=jnp.float32)
    own_cols = lax.dynamic_slice_in_dim(col_part, row_begin, local_site_number, 1)
    local_sums = lax.dynamic_update_slice_in_dim(col_part, own_cols + row_part, row_begin, 1)
    couple_amount = lax.psum(local_sums, "pos")
    focus_group_amount = jnp.sum(couple_amount, axis=1)
    combined_groups = jnp.einsum(
        "f,feg->eg", regression_factors, affinity_shares.astype(jnp.float32), precision=upper_limit
    )
    mirrored = lax.all_to_all(combined_groups, "pos", split_axis=1, concat_axis=0, tiled=True)
    slab_width = total_len // seq_count
    slab_begin = seq_index * slab_width
    resident_block = lax.dynamic_slice_in_dim(combined_groups, slab_begin, slab_width, 1)
    transposed_share = jnp.transpose(lax.dynamic_slice_in_dim(mirrored, slab_begin, slab_width, 0))
    row_factors = lax.dynamic_slice_in_dim(couple_amount, row_begin, local_site_number, 1)
    col_factors = lax.dynamic_slice_in_dim(couple_amount, slab_begin, slab_width, 1)
    product_adjuster = jnp.einsum(
        "q,qz,qd->zd",
        regression_factors / focus_group_amount,
        row_factors,
        col_factors,
        precision=upper_limit,
    )
    pairing_chances = jax.nn.sigmoid(
        resident_block + transposed_share - product_adjuster + regression_offset[0]
    )
    return (alignment_output, pairing_chances)


def solution(mesh):
    placed = (
        P("seq", "pos", None),
        P("seq", "pos", None),
        P("seq", "pos", None),
        P("seq", "pos", None),
        P(),
        P(),
        P(None, "seq"),
        P(),
        P(),
        P(),
    )
    return jax.shard_map(
        per_device,
        mesh=mesh,
        in_specs=placed,
        out_specs=(P("seq", "pos", None), P("pos", "seq")),
        check_vma=False,
    )
```

profile of v0, /device:TPU:1, one launch (start us, length us, event | category | flops | bytes accessed | tf_op | source)
XLA Modules:
  0.0 693.3 jit_solution(17357965742583726703)
XLA Ops:
  7.2 0.0 copy-start
  7.2 0.0 all-gather.4.cloned.1.call-start
  7.2 1.5 copy.50
  8.7 0.0 all-gather.4.cloned.1.call-update
  8.8 0.0 all-gather.6.cloned.1.call-start
  8.8 1.4 copy.54
  10.3 0.0 all-gather.6.cloned.1.call-update
  10.3 0.0 all-reduce.2.cloned.1.call-start
  10.3 0.9 reshape.83
  11.3 124.1 %all-gather.4.cloned.1.call-done = bf16[4,512,768]{2,0,1:T(4,128)(2,1)} async-done(((bf16[4,8,768]{2,0,1:T(4,128)(2,1)}), bf16[4,512,768]{2,0,1:T(4,128)(2,1)}) %all-gather.4.cloned.1.call-update) | async-done | bytes 3145744 | tf_op jit(solution)/shard_map/all_gather | solution.py:50
  135.4 5.9 copy.51
  141.3 3.1 fusion.8
  144.4 0.0 all-reduce.2.cloned.1.call-update
  144.4 0.0 all-gather.8.cloned.1.call-start
  144.5 0.5 all-gather.8.cloned.1.call-update
  145.6 0.0 copy-start.4
  145.7 109.3 %all-gather.6.cloned.1.call-done = bf16[4,512,768]{2,0,1:T(4,128)(2,1)} async-done(((bf16[4,8,768]{2,0,1:T(4,128)(2,1)}), bf16[4,512,768]{2,0,1:T(4,128)(2,1)}) %all-gather.6.cloned.1.call-update) | async-done | bytes 3145744 | tf_op jit(solution)/shard_map/all_gather | solution.py:62
  254.9 5.9 copy.55
  260.8 0.0 copy-start.2
  260.8 101.5 %all-reduce.2.cloned.1.call-done = f32[12,8,512]{2,1,0:T(8,128)} async-done(((f32[12,8,512]{2,1,0:T(8,128)}), f32[12,8,512]{2,1,0:T(8,128)}) %all-reduce.2.cloned.1.call-update) | async-done | bytes 196624 | tf_op jit(solution)/shard_map/psum | solution.py:58
  362.4 1.1 fusion.47
  363.5 0.2 convert_reduce_fusion
  363.7 0.0 copy-done.4
  363.7 0.2 fusion.26
  363.9 0.2 all_to_all.42
  364.1 0.0 copy-start.3
  364.1 0.8 copy.66
  364.9 14.0 %all-to-all-start.2 = ((f32[8,64,8]{2,0,1:T(8,128)}), f32[8,64,8]{2,0,1:T(8,128)S(1)}, u32[]{:S(2)}, u32[]{:S(2)}) async-start(f32[8,64,8]{2,0,1:T(8,128)} %copy.66), calls=%async_computation.2 | async-start | bytes 524288 | tf_op jit(solution)/shard_map/all_to_all | solution.py:118
  378.9 3.3 fusion.15
  382.2 0.1 copy.57
  382.3 0.1 reshape.86
  382.4 0.0 copy-done
  382.4 0.0 copy-done.2
  382.4 0.4 fusion.48
  382.9 0.2 multiply_reduce_fusion.1
  383.1 0.0 copy-done.3
  383.1 0.1 fusion.33
  383.2 0.1 dynamic-slice_add_fusion
  383.3 0.3 dynamic_update_slice.3
  383.6 267.3 %psum.15 = f32[12,512]{1,0:T(8,128)S(1)} all-reduce(f32[12,512]{1,0:T(8,128)S(1)} %dynamic_update_slice.3), channel_id=1, replica_groups=mesh['seq'=8,'pos'=64] {'pos'}, use_global_device_ids=true, to_apply=%region_8.0 | all-reduce | flops 6144 | bytes 49152 | tf_op jit(solution)/shard_map/psum | solution.py:113
  650.9 0.1 reduce_sum.69
  651.0 0.6 copy.58
  651.6 0.0 all-to-all-done.2
  651.6 6.2 all-to-all-start
  657.8 0.1 copy.78
  657.9 9.0 %all-to-all-done = bf16[4,8,768]{2,0,1:T(4,128)(2,1)S(1)} async-done(((bf16[4,8,768]{2,0,1:T(4,128)(2,1)}), bf16[4,8,768]{2,0,1:T(4,128)(2,1)S(1)}, u32[]{:S(2)}, u32[]{:S(2)}) %all-to-all-start) | async-done | bytes 49184 | tf_op jit(solution)/shard_map/all_to_all | solution.py:80
  666.9 0.0 copy-start.1
  666.9 0.0 all-gather.8.cloned.1.call-done
  666.9 3.2 convolution_convert_fusion
  670.2 0.3 reshape.89
  670.5 0.2 fusion.6
  670.7 0.2 fusion.14
  671.0 0.1 reshape.101
  671.1 0.5 broadcast.37
  671.6 0.9 reduce.3
  672.5 0.7 reshape.103
  673.2 3.3 all-to-all-start.1
  676.5 0.9 fusion.24
  677.4 8.1 %all-to-all-done.1 = bf16[8,2,1536]{2,1,0:T(2,128)(2,1)S(1)} async-done(((bf16[8,2,1536]{2,1,0:T(2,128)(2,1)}), bf16[8,2,1536]{2,1,0:T(2,128)(2,1)S(1)}, u32[]{:S(2)}, u32[]{:S(2)}) %all-to-all-start.1) | async-done | bytes 49184 | tf_op jit(solution)/shard_map/all_to_all | solution.py:96
  685.5 0.3 reduce.2
  685.8 0.0 copy-done.1
  685.9 0.9 fusion.19
  (10 shorter events, 0.2 us)
Async XLA Ops:
  7.2 375.3 %copy-start = (bf16[768,768]{1,0:T(8,128)(2,1)S(1)}, bf16[768,768]{1,0:T(8,128)(2,1)}, u32[]{:S(2)}) copy-start(bf16[768,768]{1,0:T(8,128)(2,1)} %param.14) | copy-start | bytes 3538948
  7.2 128.2 %all-gather.4.cloned.1.call-start = ((), (), s32[]{:S(2)}) async-start(), calls=%async_computation.3 | async-start | bytes 3194880 | tf_op jit(solution)/shard_map/all_gather | solution.py:50
  8.8 246.2 %all-gather.6.cloned.1.call-start = ((), (), s32[]{:S(2)}) async-start(), calls=%async_computation.5 | async-start | bytes 3194880 | tf_op jit(solution)/shard_map/all_gather | solution.py:62
  10.3 352.1 %all-reduce.2.cloned.1.call-start = ((), (), s32[]{:S(2)}) async-start(), calls=%async_computation.4 | async-start | bytes 393216 | tf_op jit(solution)/shard_map/psum | solution.py:58
  144.4 522.5 %all-gather.8.cloned.1.call-start = ((), (), s32[]{:S(2)}) async-start(), calls=%async_computation.6 | async-start | bytes 3981312 | tf_op jit(solution)/shard_map/all_gather | solution.py:77
  145.6 218.0 %copy-start.4 = (f32[12]{0:T(128)S(1)}, f32[12]{0:T(128)}, u32[]{:S(2)}) copy-start(f32[12]{0:T(128)} %param.18) | copy-start | bytes 148
  260.8 121.6 %copy-start.2 = (bf16[4,8,768]{2,1,0:T(8,128)(2,1)S(1)}, bf16[4,8,768]{2,1,0:T(8,128)(2,1)}, u32[]{:S(2)}) copy-start(bf16[4,8,768]{2,1,0:T(8,128)(2,1)} %param.10) | copy-start | bytes 147460
  364.1 19.0 %copy-start.3 = (f32[768]{0:T(1024)S(1)}, f32[768]{0:T(1024)}, u32[]{:S(2)}) copy-start(f32[768]{0:T(1024)} %param.15) | copy-start | bytes 9220
  364.9 286.7 %all-to-all-start.2 = ((f32[8,64,8]{2,0,1:T(8,128)}), f32[8,64,8]{2,0,1:T(8,128)S(1)}, u32[]{:S(2)}, u32[]{:S(2)}) async-start(f32[8,64,8]{2,0,1:T(8,128)} %copy.66), calls=%async_computation.2 | async-start | bytes 524288 | tf_op jit(solution)/shard_map/all_to_all | solution.py:118
  651.6 15.2 %all-to-all-start = ((bf16[4,8,768]{2,0,1:T(4,128)(2,1)}), bf16[4,8,768]{2,0,1:T(4,128)(2,1)S(1)}, u32[]{:S(2)}, u32[]{:S(2)}) async-start(bf16[4,8,768]{2,0,1:T(4,128)(2,1)} %copy.58), calls=%async_computation | async-start | bytes 98304 | tf_op jit(solution)/shard_map/all_to_all | solution.py:80
  666.9 19.0 %copy-start.1 = (bf16[768,768]{1,0:T(8,128)(2,1)S(1)}, bf16[768,768]{1,0:T(8,128)(2,1)}, u32[]{:S(2)}) copy-start(bf16[768,768]{1,0:T(8,128)(2,1)} %param.17) | copy-start | bytes 3538948
  673.2 12.3 %all-to-all-start.1 = ((bf16[8,2,1536]{2,1,0:T(2,128)(2,1)}), bf16[8,2,1536]{2,1,0:T(2,128)(2,1)S(1)}, u32[]{:S(2)}, u32[]{:S(2)}) async-start(bf16[8,2,1536]{2,1,0:T(2,128)(2,1)} %reshape.103), calls=%async_computation.1 | async-start | bytes 98304 | tf_op jit(solution)/shard_map/all_to_all | solution.py:96
Sparse Core Ops, SparseCore 0:
  10.1 125.2 all-gather.3
  138.1 116.7 all-gather.5
  257.8 104.4 all-reduce.1
  365.4 103.7 all-gather.7
where the time goes:
time: 701 us; the launch traced here: 693 us
  waiting for transfers between devices  353 us (50%)
  blocking collectives  267 us (38%)
  starting transfers between devices  23.7 us (3%)
  local copies, waits for them, and re-layouts  19.5 us (3%)
  between operations  14.6 us (2%)
  matrix products  12.6 us (2%)
    psum x1, blocking collectives, per_device(): couple_amount = lax.psum(local_sums, 'pos')  267 us
    all_gather x1, waiting for transfers between devices, per_device(): lax.all_gather(lateral_matched_vectors, 'pos', axis=1, tiled=True)  124 us
    all_gather x1, waiting for transfers between devices, per_device(): lax.all_gather(lateral_carried_vectors, 'pos', axis=1, tiled=True)  109 us
    psum x1, waiting for transfers between devices, per_device(): logits = lax.psum(partial_value, 'seq') * factor  102 us
  transfers between devices with their start and end apart: 7, of which 5 were waited for; matrix products, arithmetic and copies ran while one was open for 4% of the time, Pallas kernels for 0%

commit v1 on v0

v1 whole, which is shorter than its diff:
```python
import math

import jax
import jax.numpy as jnp
from jax import lax
from jax.experimental import pallas as pl
from jax.experimental.pallas import tpu as pltpu
from jax.sharding import PartitionSpec as P

MESH = pl.DeviceIdType.MESH
HI = lax.Precision.HIGHEST
F32 = jnp.float32
BF16 = jnp.bfloat16
NT = (((1,), (1,)), ((), ()))
CHUNKS = 2


def body(
    skip_hbm, q_hbm, k_hbm, v_hbm, wc_hbm, gain_ref, w3_hbm, wo_hbm, factor_ref, offset_ref,
    out_ref, pair_ref,
    qg, kg, vg, wb, wc, wo, sk,
    part, rs, wm, wg, wf, nf, nm, ng, cm, cg, hid, proj,
    ptl, ptz, pty, pts, mloc, mrow, mcol, stage,
    lsem, ssem, rq, rqs, rk, rva, rvs, rvr, rwx, rww, rrs, rwg, rng, rcg, rpz, rpy, rps, rm1, rm2,
):
    s = lax.axis_index("seq")
    p = lax.axis_index("pos")
    x, zh = s // 2, s % 2
    y, zc = p // 8, p % 8
    zl, c = zc // 2, zc % 2
    sib = y * 8 + zl * 2 + (1 - c)
    partner = x * 2 + (1 - zh)

    def local(src, dst, index):
        copy = pltpu.make_async_copy(src, dst, lsem.at[index])
        copy.start()
        return copy

    def send(src, dst, send_sem, recv_sem, seq, pos):
        pltpu.make_async_remote_copy(
            src_ref=src, dst_ref=dst, send_sem=send_sem, recv_sem=recv_sem,
            device_id=(seq, pos), device_id_type=MESH,
        ).start()

    def wait(ref, sem):
        pltpu.make_async_copy(ref, ref, sem).wait()

    loads = [
        local(q_hbm, qg.at[zc], 0),
        local(k_hbm, kg.at[y], 1),
        local(v_hbm, vg.at[c, y, zl], 2),
        local(w3_hbm, wb.at[s], 3),
        local(wc_hbm, wc, 4),
        local(wo_hbm, wo, 5),
        local(skip_hbm, sk, 6),
    ]

    barrier = pltpu.get_barrier_semaphore()
    plane = s * 8 + zc

    def greet(d, carry):
        o = (plane + d) % 64
        pl.semaphore_signal(barrier, inc=1, device_id=(o // 8, y * 8 + o % 8), device_id_type=MESH)
        return carry

    lax.fori_loop(1, 64, greet, 0)
    for d in range(1, 8):
        pl.semaphore_signal(
            barrier, inc=1, device_id=(s, ((y + d) % 8) * 8 + zc), device_id_type=MESH
        )
    pl.semaphore_wait(barrier, 70)

    y_order = (1, 7, 2, 6, 3, 5, 4)
    send(q_hbm, qg.at[zc], ssem.at[0], rqs.at[zl], s, sib)
    for d in (1, 3, 2):
        send(q_hbm, qg.at[zc], ssem.at[1], rq.at[zl], s, y * 8 + ((zl + d) % 4) * 2 + c)
    for d in y_order:
        send(k_hbm, kg.at[y], ssem.at[2], rk, s, ((y + d) % 8) * 8 + zc)
    for d in (1, 3, 2):
        send(v_hbm, vg.at[c, y, zl], ssem.at[3], rva, s, y * 8 + ((zl + d) % 4) * 2 + c)

    rows = 384 // CHUNKS

    def w_rows(ch):
        return pl.ds(pl.multiple_of(c * 384 + ch * rows, rows), rows)

    def w_own(ch):
        for d in (1, 3, 2):
            send(
                w3_hbm.at[w_rows(ch), :], wb.at[s, w_rows(ch), :], ssem.at[4 + ch],
                rwx.at[ch, (4 - d) % 4], ((x + d) % 4) * 2 + zh, p,
            )

    def w_over(ch):
        send(
            w3_hbm.at[w_rows(ch), :], wb.at[s, w_rows(ch), :], ssem.at[6 + ch],
            rwx.at[ch, 4], partner, p,
        )

    def w_relay(ch):
        wait(wb.at[partner, w_rows(ch), :], rwx.at[ch, 4])
        for d in (1, 3, 2):
            send(
                wb.at[partner, w_rows(ch), :], wb.at[partner, w_rows(ch), :], ssem.at[8 + ch],
                rwx.at[ch, 4 + (4 - d) % 4], ((x + d) % 4) * 2 + zh, p,
            )
        send(
            wb.at[partner, w_rows(ch), :], wb.at[partner, w_rows(ch), :], ssem.at[10],
            rww, s, sib,
        )

    def w_sibling(ch, far):
        for d in (1, 3, 2):
            shard = ((x + d) % 4) * 2 + (partner % 2 if far else zh)
            wait(wb.at[shard, w_rows(ch), :], rwx.at[ch, (4 if far else 0) + d])
            send(
                wb.at[shard, w_rows(ch), :], wb.at[shard, w_rows(ch), :], ssem.at[10],
                rww, s, sib,
            )

    for ch in range(CHUNKS):
        w_own(ch)
    w_over(0)

    part[:, 6:8, :] = jnp.zeros((64, 2, 128), F32)

    for d in (1, 3, 2):
        other = (zl + d) % 4
        wait(qg.at[0], rq.at[other])
        send(
            qg.at[other * 2 + c], qg.at[other * 2 + c], ssem.at[0], rqs.at[other], s, sib
        )
    loads[0].wait()
    loads[1].wait()
    for other in range(4):
        wait(qg.at[0], rqs.at[other])
    wait(kg.at[0:7], rk)

    lane64 = lax.broadcasted_iota(jnp.int32, (64, 128), 1) < 64
    zero64 = jnp.zeros((64, 128), BF16)
    for k in range(6):
        left = jnp.concatenate([qg[:, r, k].reshape(64, 128) for r in range(4)], axis=1)
        keys = [kg[:, r, k].reshape(64, 128) for r in range(4)]
        low = jnp.concatenate([jnp.where(lane64, b, zero64) for b in keys], axis=1)
        high = jnp.concatenate([jnp.where(lane64, zero64, b) for b in keys], axis=1)
        tile = lax.dot_general(
            left, jnp.concatenate([low, high], axis=0), NT, preferred_element_type=F32
        )
        part[:, k, :] = tile

    own = pltpu.make_async_copy(part.at[zc * 8 + s], rs.at[plane], lsem.at[7])
    own.start()

    def scatter(d, carry):
        o = (plane + d) % 64
        so, zo = o // 8, o % 8
        send(part.at[zo * 8 + so], rs.at[plane], ssem.at[11], rrs, so, y * 8 + zo)
        return carry

    lax.fori_loop(1, 64, scatter, 0)

    up, down = ((y + 1) % 8) * 8 + zc, ((y + 7) % 8) * 8 + zc

    def v_send(block, step, halves):
        if halves:
            send(
                vg.at[c, block[0], 0:2], vg.at[c, block[0], 0:2], ssem.at[12], rvr.at[0, step], s, up
            )
            send(
                vg.at[c, block[1], 2:4], vg.at[c, block[1], 2:4], ssem.at[12], rvr.at[1, step], s, down
            )
            return
        send(vg.at[c, block[0]], vg.at[c, block[0]], ssem.at[13], rvr.at[0, step], s, up)
        send(vg.at[c, block[1]], vg.at[c, block[1]], ssem.at[13], rvr.at[1, step], s, down)

    def v_sib(block):
        send(vg.at[c, block], vg.at[c, block], ssem.at[14], rvs, s, sib)

    loads[2].wait()
    wait(vg.at[0, 0, 0:3], rva)
    v_send((y, y), 0, False)
    v_sib(y)

    def v_step(step):
        below, above = (y + 8 - step) % 8, (y + step) % 8
        wait(vg.at[0, 0], rvr.at[0, step - 1])
        wait(vg.at[0, 0], rvr.at[1, step - 1])
        v_send((below, above), step, step == 3)
        v_sib(below)
        v_sib(above)

    v_step(1)

    own.wait()
    wait(rs.at[0:63], rrs)
    logits = rs[0:8]
    for so in range(1, 8):
        logits = logits + rs[so * 8 : so * 8 + 8]
    logits = logits * (1.0 / (math.sqrt(64) * math.sqrt(32)))
    lane8 = lax.broadcasted_iota(jnp.int32, (8, 128), 1)
    lower = lane8 < 64
    peak = jnp.max(logits, axis=0)
    neg = jnp.full((8, 128), -jnp.inf, F32)
    peak_low = jnp.max(jnp.where(lower, peak, neg), axis=1, keepdims=True)
    peak_high = jnp.max(jnp.where(lower, neg, peak), axis=1, keepdims=True)
    exponent = jnp.exp(logits - jnp.where(lower, peak_low, peak_high)[None])
    total = jnp.sum(exponent, axis=0)
    zero8 = jnp.zeros((8, 128), F32)
    total_low = jnp.sum(jnp.where(lower, total, zero8), axis=1, keepdims=True)
    total_high = jnp.sum(jnp.where(lower, zero8, total), axis=1, keepdims=True)
    weights = exponent / jnp.where(lower, total_low, total_high)[None]
    for z in range(4):
        even, odd = weights[2 * z], weights[2 * z + 1]
        wm[z] = jnp.where(lower, even, pltpu.roll(odd, 64, 1)).astype(BF16)
        wm[4 + z] = jnp.where(lower, pltpu.roll(even, 64, 1), odd).astype(BF16)

    seq_order = (7, 1, 2, 6, 3, 5, 4)
    keep = pltpu.make_async_copy(wm, wg.at[s], lsem.at[8])
    keep.start()
    for d in seq_order:
        send(wm, wg.at[s], ssem.at[15], rwg, (s + d) % 8, p)
    for ch in range(1, CHUNKS):
        w_over(ch)

    for step in (2, 3):
        v_step(step)
    w_relay(0)

    keep.wait()
    wait(wg.at[0:7], rwg)
    wf[...] = wg[...].astype(F32)

    sums = wf[0]
    for i in range(1, 8):
        sums = sums + wf[i]
    base = c * 64 + y * 8
    for hh in range(2):
        placed = zero8
        for i in range(8):
            block = wf[i, hh * 4] + wf[i, hh * 4 + 1] + wf[i, hh * 4 + 2] + wf[i, hh * 4 + 3]
            placed = placed + jnp.where(
                lane8 == base + i, jnp.sum(block, axis=1, keepdims=True), zero8
            )
        for z in range(4):
            here = (zl == z).astype(F32)
            ptl[hh * 4 + z] = sums[hh * 4 + z] + here * placed
    ptz[zc] = ptl[s]
    for d in range(1, 8):
        send(ptl.at[s], ptz.at[zc], ssem.at[16], rpz, s, y * 8 + (zc + d) % 8)

    for z in range(4):
        acc = zero8
        for k in range(6):
            for hh in range(2):
                acc = acc + factor_ref[2 * k + hh] * wf[:, hh * 4 + z, k, :]
        mloc[z] = acc

    @pl.when(y == s)
    def _():
        for d in y_order:
            send(mloc, mrow, ssem.at[17], rm1, s, ((y + d) % 8) * 8 + zc)

    for step in (3,):
        wait(vg.at[0, 0, 0:2], rvr.at[0, step])
        wait(vg.at[0, 0, 2:4], rvr.at[1, step])
    opposite = (y + 4) % 8
    v_sib(opposite)
    wait(vg.at[0], rvs)

    lower16 = lax.broadcasted_iota(jnp.int32, (8, 512), 1) % 128 < 64
    mixed = []
    for k in range(6):
        left = jnp.concatenate(
            [
                jnp.concatenate([wf[:, hh * 4 + z, k, :] for z in range(4)], axis=1)
                for hh in range(2)
            ],
            axis=0,
        ).astype(BF16)
        right = jnp.concatenate(
            [
                jnp.concatenate(
                    [vg[:, :, z, r, k].reshape(128, 128) for z in range(4)], axis=0
                )
                for r in range(4)
            ],
            axis=1,
        )
        both = jnp.dot(left, right, preferred_element_type=F32)
        mixed.append(jnp.where(lower16, both[0:8], both[8:16]))
    row_out = jnp.concatenate(
        [
            jnp.concatenate([mixed[k][:, r * 128 : r * 128 + 128] for k in range(6)], axis=1)
            for r in range(4)
        ],
        axis=0,
    ).astype(BF16)
    loads[4].wait()
    loads[6].wait()
    skip = jnp.concatenate(
        [
            jnp.concatenate([sk[r, k].astype(F32) for k in range(6)], axis=1)
            for r in range(4)
        ],
        axis=0,
    )
    hidden = skip + jnp.dot(row_out, wc[...], preferred_element_type=F32)
    hid[...] = hidden
    average = jnp.mean(hidden, axis=1, keepdims=True)
    centered = hidden - average
    spread = jnp.mean(centered * centered, axis=1, keepdims=True)
    normed = centered * lax.rsqrt(spread + 1e-05) * gain_ref[...]
    for r in range(4):
        for k in range(6):
            nf[:, r * 6 + k, :] = normed[r * 8 : r * 8 + 8, k * 128 : k * 128 + 128]
    nm[...] = nf[...].astype(BF16)
    keep = pltpu.make_async_copy(nm.at[s], ng.at[s], lsem.at[9])
    keep.start()
    for d in seq_order:
        send(nm.at[(s + d) % 8], ng.at[s], ssem.at[18], rng, (s + d) % 8, p)

    for ch in range(1, CHUNKS):
        w_relay(ch)
    for ch in range(CHUNKS):
        w_sibling(ch, False)

    wait(ptz.at[0:7], rpz)
    acc = ptz[0]
    for z in range(1, 8):
        acc = acc + ptz[z]
    stage[0] = acc
    pty[y] = acc
    for d in y_order:
        send(stage.at[0], pty.at[y], ssem.at[19], rpy, s, ((y + d) % 8) * 8 + zc)
    for ch in range(CHUNKS):
        w_sibling(ch, True)
    loads[3].wait()
    wait(wb.at[0:7, 0:384, :], rww)

    def unpack(ref):
        nf[...] = ref[...].astype(F32)
        return jnp.concatenate(
            [
                jnp.concatenate([nf[:, r * 6 + k, :] for k in range(6)], axis=1)
                for r in range(4)
            ],
            axis=0,
        ).astype(BF16)

    keep.wait()
    wait(ng.at[0:7], rng)
    cells = unpack(ng)
    for so in range(8):
        proj[:, so * 288 : so * 288 + 288] = jnp.dot(
            cells, wb[so], preferred_element_type=F32
        )
    lane32 = lax.broadcasted_iota(jnp.int32, (32, 128), 1) < 64
    zero32 = jnp.zeros((32, 128), BF16)
    outs = []
    for k in range(6):
        cq = proj[:, k * 128 : k * 128 + 128].astype(BF16)
        ck = proj[:, 768 + k * 128 : 768 + k * 128 + 128].astype(BF16)
        cv = proj[:, 1536 + k * 128 : 1536 + k * 128 + 128].astype(BF16)
        left = jnp.concatenate(
            [jnp.where(lane32, cq, zero32), jnp.where(lane32, zero32, cq)], axis=0
        )
        score = lax.dot_general(left, ck, NT, preferred_element_type=F32) * (1.0 / math.sqrt(64))
        exponent = jnp.exp(score)
        share = (exponent / jnp.sum(exponent, axis=1, keepdims=True)).astype(BF16)
        both = jnp.dot(share, cv, preferred_element_type=F32)
        outs.append(jnp.where(lane32, both[0:32], both[32:64]))
    for r in range(4):
        for k in range(6):
            nf[:, r * 6 + k, :] = outs[k][r * 8 : r * 8 + 8]
    cm[...] = nf[...].astype(BF16)
    keep = pltpu.make_async_copy(cm.at[s], cg.at[s], lsem.at[10])
    keep.start()
    for d in seq_order:
        send(cm.at[(s + d) % 8], cg.at[s], ssem.at[20], rcg, (s + d) % 8, p)

    wait(pty.at[0:7], rpy)
    acc = pty[0]
    for o in range(1, 8):
        acc = acc + pty[o]
    stage[1] = acc
    pts[s] = acc
    for d in seq_order:
        send(stage.at[1], pts.at[s], ssem.at[21], rps, (s + d) % 8, p)

    @pl.when(y == s)
    def _():
        mrow[...] = mloc[...]

    @pl.when(y != s)
    def _():
        wait(mrow, rm1)

    mcol[zc] = mrow[zl]
    for d in range(1, 8):
        o = (zc + d) % 8
        send(mrow.at[o // 2], mcol.at[zc], ssem.at[22], rm2, s, y * 8 + o)

    loads[5].wait()
    keep.wait()
    wait(cg.at[0:7], rcg)
    cells = unpack(cg)
    closing = hid[...] + jnp.dot(cells, wo[...], preferred_element_type=F32)
    for r in range(4):
        for k in range(6):
            out_ref[r, k] = closing[r * 8 : r * 8 + 8, k * 128 : k * 128 + 128].astype(BF16)

    wait(pts.at[0:7], rps)
    wait(mcol.at[0:7], rm2)
    row8 = lax.broadcasted_iota(jnp.int32, (8, 128), 0)
    scaled, cols = [], []
    for hh in range(2):
        whole = pts[hh * 4] + pts[hh * 4 + 1] + pts[hh * 4 + 2] + pts[hh * 4 + 3]
        head_total = jnp.sum(whole, axis=1, keepdims=True)
        factor = zero8
        for k in range(6):
            factor = jnp.where(row8 == k, factor_ref[2 * k + hh], factor)
        scaled.append(factor / head_total * pts[hh * 4 + zl])
    block = jnp.zeros((24, 64), F32)
    lane_at = lax.broadcasted_iota(jnp.int32, (128, 64), 0)
    col_at = lax.broadcasted_iota(jnp.int32, (128, 64), 1)
    wanted = ((col_at // 8) % 2) * 64 + s * 8 + col_at % 8
    for z in range(4):
        pick = jnp.where((lane_at == wanted) & (col_at // 16 == z), 1.0, 0.0).astype(F32)
        block = block + jnp.dot(
            jnp.concatenate([pts[z], pts[4 + z], mloc[z]], axis=0), pick,
            precision=HI, preferred_element_type=F32,
        )
    mine = jnp.where(lane8 == base + row8, 1.0, 0.0).astype(F32)
    rows_here = lax.dot_general(
        mine, jnp.concatenate(scaled, axis=0), NT, precision=HI, preferred_element_type=F32
    )
    product = jnp.dot(rows_here, block[0:16], precision=HI, preferred_element_type=F32)
    mirrored = lax.dot_general(
        mine, mcol[...].reshape(64, 128), NT, precision=HI, preferred_element_type=F32
    )
    pair_ref[...] = jax.nn.sigmoid(block[16:24] + mirrored - product + offset_ref[0])

    wait(qg.at[0:4], ssem.at[0])
    wait(qg.at[0:3], ssem.at[1])
    wait(kg.at[0:7], ssem.at[2])
    wait(vg.at[0, 0, 0:3], ssem.at[3])
    for ch in range(CHUNKS):
        wait(wb.at[0:3, 0:rows, :], ssem.at[4 + ch])
        wait(wb.at[0, 0:rows, :], ssem.at[6 + ch])
        wait(wb.at[0:3, 0:rows, :], ssem.at[8 + ch])
    wait(wb.at[0:7, 0:384, :], ssem.at[10])
    wait(rs.at[0:63], ssem.at[11])
    wait(vg.at[0, 0], ssem.at[12])
    wait(vg.at[0, 0:6], ssem.at[13])
    wait(vg.at[0], ssem.at[14])
    wait(wg.at[0:7], ssem.at[15])
    wait(ptz.at[0:7], ssem.at[16])

    @pl.when(y == s)
    def _():
        wait(rs.at[0:28], ssem.at[17])

    wait(ng.at[0:7], ssem.at[18])
    wait(pty.at[0:7], ssem.at[19])
    wait(cg.at[0:7], ssem.at[20])
    wait(pts.at[0:7], ssem.at[21])
    wait(mcol.at[0:7], ssem.at[22])


def per_device(
    skip_stream_input,
    lateral_asking_vectors,
    lateral_matched_vectors,
    lateral_carried_vectors,
    lateral_closing_linear,
    upright_normalizer_multiplier,
    upright_threefold_linear,
    upright_closing_linear,
    regression_factors,
    regression_offset,
):
    def tiles(array):
        return array.reshape(4, 8, 6, 128).transpose(0, 2, 1, 3)

    def vmem(*shape, dtype=BF16):
        return pltpu.VMEM(shape, dtype)

    def dma(*shape):
        return pltpu.SemaphoreType.DMA(shape)

    anywhere = pl.BlockSpec(memory_space=pl.ANY)
    in_vmem = pl.BlockSpec(memory_space=pltpu.VMEM)
    in_smem = pl.BlockSpec(memory_space=pltpu.SMEM)
    one = pltpu.SemaphoreType.DMA
    aligned, pairs = pl.pallas_call(
        body,
        out_shape=(
            jax.ShapeDtypeStruct((4, 6, 8, 128), BF16),
            jax.ShapeDtypeStruct((8, 64), F32),
        ),
        in_specs=[
            anywhere, anywhere, anywhere, anywhere, anywhere, in_vmem, anywhere, anywhere,
            in_smem, in_smem,
        ],
        out_specs=(in_vmem, in_vmem),
        scratch_shapes=[
            vmem(8, 4, 6, 8, 128),
            vmem(8, 4, 6, 8, 128),
            vmem(2, 8, 4, 4, 6, 8, 128),
            vmem(8, 768, 288),
            vmem(768, 768),
            vmem(768, 768),
            vmem(4, 6, 8, 128),
            vmem(64, 8, 128, dtype=F32),
            vmem(64, 8, 128, dtype=F32),
            vmem(8, 8, 128),
            vmem(8, 8, 8, 128),
            vmem(8, 8, 8, 128, dtype=F32),
            vmem(8, 24, 128, dtype=F32),
            vmem(8, 24, 128),
            vmem(8, 24, 128),
            vmem(8, 24, 128),
            vmem(8, 24, 128),
            vmem(32, 768, dtype=F32),
            vmem(32, 2304, dtype=F32),
            vmem(8, 8, 128, dtype=F32),
            vmem(8, 8, 128, dtype=F32),
            vmem(8, 8, 128, dtype=F32),
            vmem(8, 8, 128, dtype=F32),
            vmem(4, 8, 128, dtype=F32),
            vmem(4, 8, 128, dtype=F32),
            vmem(8, 8, 128, dtype=F32),
            vmem(2, 8, 128, dtype=F32),
            dma(11),
            dma(23),
            dma(4),
            dma(4),
            one,
            one,
            one,
            dma(2, 4),
            dma(CHUNKS, 8),
            one,
            one,
            one,
            one,
            one,
            one,
            one,
            one,
            one,
            one,
        ],
        compiler_params=pltpu.CompilerParams(
            collective_id=0, has_side_effects=True, vmem_limit_bytes=48 << 20
        ),
        name="axial_layer",
    )(
        tiles(skip_stream_input),
        tiles(lateral_asking_vectors),
        tiles(lateral_matched_vectors),
        tiles(lateral_carried_vectors),
        lateral_closing_linear,
        upright_normalizer_multiplier.reshape(1, 768),
        upright_threefold_linear,
        upright_closing_linear,
        regression_factors,
        regression_offset,
    )
    return aligned.transpose(0, 2, 1, 3).reshape(4, 8, 768), pairs


def solution(mesh):
    placed = (
        P("seq", "pos", None),
        P("seq", "pos", None),
        P("seq", "pos", None),
        P("seq", "pos", None),
        P(),
        P(),
        P(None, "seq"),
        P(),
        P(),
        P(),
    )
    return jax.shard_map(
        per_device,
        mesh=mesh,
        in_specs=placed,
        out_specs=(P("seq", "pos", None), P("pos", "seq")),
        check_vma=False,
    )
```

time: 701 us -> 93 us (0.13); the launches traced: 693 us -> 92.4 us
  waiting for transfers between devices: 353 us -> 0 us
  blocking collectives: 267 us -> 0 us
  Pallas kernels: 0 us -> 81.5 us
  starting transfers between devices: 23.7 us -> 0 us
  between operations: 14.6 us -> 1.3 us
  matrix products: 12.6 us -> 0 us
  local copies, waits for them, and re-layouts: 19.5 us -> 9.6 us
    psum x1 -> x0, blocking collectives: 267 us -> none  [per_device(): couple_amount = lax.psum(local_sums, 'pos')]
    all_gather x3 -> x0, waiting for transfers between devices: 233 us -> none  [the longest x1 124 us: per_device(): lax.all_gather(lateral_matched_vectors, 'pos', axis=1, tiled=True)]
    psum x1 -> x0, waiting for transfers between devices: 102 us -> none  [per_device(): logits = lax.psum(partial_value, 'seq') * factor]
    pallas_call x0 -> x1, Pallas kernels: none -> 81.5 us  [per_device(): pl.pallas_call(body, out_shape=(jax.ShapeDtypeStruct((4, 6, 8, 128), BF16...]
    all_to_all x3 -> x0, starting transfers between devices: 23.5 us -> none  [the longest x1 14 us: per_device(): lax.all_to_all(combined_groups, 'pos', split_axis=1, concat_axis=0, tiled...]
    all_to_all x3 -> x0, waiting for transfers between devices: 17.1 us -> none  [the longest x1 8.99 us: per_device(): lax.all_to_all(normed.reshape(local_homolog_number, local_site_number, em...]
    dot_general x9 -> x0, matrix products: 12.6 us -> none  [the longest x1 3.31 us: per_device(): jnp.einsum('hij,rjhd->rihd', affinity_shares, value_part, preferred_eleme...]
    all_gather x2 -> x0, local copies, waits for them, and re-layouts: 11.7 us -> none  [the longest x1 5.86 us: per_device(): lax.all_gather(lateral_matched_vectors, 'pos', axis=1, tiled=True)]
  transfers between devices with their start and end apart: 7 -> 0, of which waited for: 5 -> 0; matrix products, arithmetic and copies ran while one was open for 4% -> 0% of each run, Pallas kernels for 0% -> 0%
where the time goes in v1:
time: 93 us; the launch traced here: 92.4 us
  Pallas kernels  81.5 us (88%)
  local copies, waits for them, and re-layouts  9.6 us (10%)
  between operations  1.3 us (1%)
    pallas_call x1, Pallas kernels, per_device(): pl.pallas_call(body, out_shape=(jax.ShapeDtypeStruct((4, 6, 8, 128), BF16...  81.5 us
    unnamed x17, local copies, waits for them, and re-layouts  8.91 us

profile of v1, /device:TPU:1, one launch (start us, length us, event | category | flops | bytes accessed | tf_op | source)
XLA Modules:
  0.0 92.4 jit_solution(10485342147958997340)
XLA Ops:
  1.3 0.7 reshape.26.gain_ref
  2.0 1.3 %copy.12.w3_hbm = bf16[768,288]{1,0:T(8,128)(2,1)S(1)} copy(bf16[768,288]{0,1:T(8,128)(2,1)} %param.16) | data formatting | bytes 884736 | tf_op args[6]
  3.3 0.0 copy-start
  3.3 1.3 %copy-done = bf16[768,768]{1,0:T(8,128)(2,1)S(1)} copy-done((bf16[768,768]{1,0:T(8,128)(2,1)S(1)}, bf16[768,768]{1,0:T(8,128)(2,1)}, u32[]{:S(2)}) %copy-start) | copy-done | bytes 1179672
  4.6 0.0 copy-start.1
  4.6 1.3 %copy-done.1 = bf16[768,768]{1,0:T(8,128)(2,1)S(1)} copy-done((bf16[768,768]{1,0:T(8,128)(2,1)S(1)}, bf16[768,768]{1,0:T(8,128)(2,1)}, u32[]{:S(2)}) %copy-start.1) | copy-done | bytes 1179672
  5.8 0.0 copy-start.2
  5.8 0.8 copy-done.2
  6.6 0.0 copy-start.3
  6.6 0.8 copy-done.3
  7.4 0.0 copy-start.4
  7.4 0.8 copy-done.4
  8.2 0.0 copy-start.5
  8.2 0.8 copy-done.5
  9.0 0.0 copy-start.6
  9.0 0.7 copy-done.6
  9.7 81.5 %axial_layer.1 = (bf16[4,6,8,128]{3,2,1,0:T(8,128)(2,1)S(1)}, f32[8,64]{1,0:T(8,128)S(1)}) custom-call(bf16[4,6,8,128]{3,2,1,0:T(8,128)(2,1)S(1)} %bitcast.16, bf16[4,6,8,128]{3,2,1,0:T(8,128)(2,1)S(1)} %bitcast.17, bf16[4,6,8,128]{3,2,1,0:T(8,128)(2,1)S(1)} %bitcast.18, bf16[4,6,8,128]{3,2,1,0:T(8,128)(2,1)S(1)} %bitcast.19, bf16[768,768]{1,0:T(8,128)(2,1)S(1)} %copy-done, ...), custom_call_target="tpu_custom_call" | custom-call | tf_op jit(solution)/shard_map/axial_layer/pallas_call | solution.py:495
  91.2 0.6 copy.16
  91.8 0.6 copy.17
Async XLA Ops:
  3.3 1.3 %copy-start = (bf16[768,768]{1,0:T(8,128)(2,1)S(1)}, bf16[768,768]{1,0:T(8,128)(2,1)}, u32[]{:S(2)}) copy-start(bf16[768,768]{1,0:T(8,128)(2,1)} %wc_hbm.1) | copy-start | bytes 3538948
  4.6 1.3 %copy-start.1 = (bf16[768,768]{1,0:T(8,128)(2,1)S(1)}, bf16[768,768]{1,0:T(8,128)(2,1)}, u32[]{:S(2)}) copy-start(bf16[768,768]{1,0:T(8,128)(2,1)} %wo_hbm.1) | copy-start | bytes 3538948
  5.8 0.8 copy-start.2
  6.6 0.8 copy-start.3
  7.4 0.8 copy-start.4
  8.2 0.8 copy-start.5
  9.0 0.7 copy-start.6

commit v2 on v1

--- a/solution.py
+++ b/solution.py
@@ -13,13 +13,14 @@
 BF16 = jnp.bfloat16
 NT = (((1,), (1,)), ((), ()))
 CHUNKS = 2
+W_AT, W_ROWS = (0, 80), (80, 64)
 
 
 def body(
-    skip_hbm, q_hbm, k_hbm, v_hbm, wc_hbm, gain_ref, w3_hbm, wo_hbm, factor_ref, offset_ref,
+    skip_hbm, q_hbm, k_hbm, v_hbm, wc_hbm, gain_hbm, w3_hbm, wo_hbm, factor_hbm, offset_ref,
     out_ref, pair_ref,
     qg, kg, vg, wb, wc, wo, sk,
-    part, rs, wm, wg, wf, nf, nm, ng, cm, cg, hid, proj,
+    part, rs, wm, wg, wf, nf, nm, ng, cm, cg, hid, proj, gain, factor_ref,
     ptl, ptz, pty, pts, mloc, mrow, mcol, stage,
     lsem, ssem, rq, rqs, rk, rva, rvs, rvr, rwx, rww, rrs, rwg, rng, rcg, rpz, rpy, rps, rm1, rm2,
 ):
@@ -49,72 +50,76 @@
         local(q_hbm, qg.at[zc], 0),
         local(k_hbm, kg.at[y], 1),
         local(v_hbm, vg.at[c, y, zl], 2),
-        local(w3_hbm, wb.at[s], 3),
+        local(w3_hbm, wb.at[pl.ds(pl.multiple_of(s * 288, 16), 288), :], 3),
         local(wc_hbm, wc, 4),
         local(wo_hbm, wo, 5),
         local(skip_hbm, sk, 6),
+        local(gain_hbm, gain, 11),
+        local(factor_hbm, factor_ref, 12),
     ]
 
     barrier = pltpu.get_barrier_semaphore()
     plane = s * 8 + zc
 
-    def greet(d, carry):
-        o = (plane + d) % 64
-        pl.semaphore_signal(barrier, inc=1, device_id=(o // 8, y * 8 + o % 8), device_id_type=MESH)
-        return carry
-
-    lax.fori_loop(1, 64, greet, 0)
+    for d in range(1, 64):
+        pl.semaphore_signal(
+            barrier, inc=1, device_id=((s + d // 8) % 8, y * 8 + (zc + d % 8) % 8), device_id_type=MESH
+        )
     for d in range(1, 8):
         pl.semaphore_signal(
             barrier, inc=1, device_id=(s, ((y + d) % 8) * 8 + zc), device_id_type=MESH
         )
     pl.semaphore_wait(barrier, 70)
 
-    y_order = (1, 7, 2, 6, 3, 5, 4)
+    y_order = (4, 3, 5, 2, 6, 1, 7)
     send(q_hbm, qg.at[zc], ssem.at[0], rqs.at[zl], s, sib)
     for d in (1, 3, 2):
         send(q_hbm, qg.at[zc], ssem.at[1], rq.at[zl], s, y * 8 + ((zl + d) % 4) * 2 + c)
     for d in y_order:
         send(k_hbm, kg.at[y], ssem.at[2], rk, s, ((y + d) % 8) * 8 + zc)
+    up, down = ((y + 1) % 8) * 8 + zc, ((y + 7) % 8) * 8 + zc
     for d in (1, 3, 2):
-        send(v_hbm, vg.at[c, y, zl], ssem.at[3], rva, s, y * 8 + ((zl + d) % 4) * 2 + c)
-
-    rows = 384 // CHUNKS
-
-    def w_rows(ch):
-        return pl.ds(pl.multiple_of(c * 384 + ch * rows, rows), rows)
+        send(v_hbm, vg.at[c, y, zl], ssem.at[3], rva.at[zl], s, y * 8 + ((zl + d) % 4) * 2 + c)
+    send(v_hbm, vg.at[c, y, zl], ssem.at[13], rvr.at[0, 0, zl], s, up)
+    send(v_hbm, vg.at[c, y, zl], ssem.at[13], rvr.at[1, 0, zl], s, down)
+
+    def w_rows(shard, ch):
+        return pl.ds(pl.multiple_of(shard * 288 + c * 144 + W_AT[ch], 16), W_ROWS[ch])
+
+    def w_src(ch):
+        return w3_hbm.at[pl.ds(pl.multiple_of(c * 144 + W_AT[ch], 16), W_ROWS[ch]), :]
 
     def w_own(ch):
         for d in (1, 3, 2):
             send(
-                w3_hbm.at[w_rows(ch), :], wb.at[s, w_rows(ch), :], ssem.at[4 + ch],
+                w_src(ch), wb.at[w_rows(s, ch), :], ssem.at[4 + ch],
                 rwx.at[ch, (4 - d) % 4], ((x + d) % 4) * 2 + zh, p,
             )
 
     def w_over(ch):
         send(
-            w3_hbm.at[w_rows(ch), :], wb.at[s, w_rows(ch), :], ssem.at[6 + ch],
+            w_src(ch), wb.at[w_rows(s, ch), :], ssem.at[6 + ch],
             rwx.at[ch, 4], partner, p,
         )
 
     def w_relay(ch):
-        wait(wb.at[partner, w_rows(ch), :], rwx.at[ch, 4])
+        wait(wb.at[w_rows(partner, ch), :], rwx.at[ch, 4])
         for d in (1, 3, 2):
             send(
-                wb.at[partner, w_rows(ch), :], wb.at[partner, w_rows(ch), :], ssem.at[8 + ch],
+                wb.at[w_rows(partner, ch), :], wb.at[w_rows(partner, ch), :], ssem.at[8 + ch],
                 rwx.at[ch, 4 + (4 - d) % 4], ((x + d) % 4) * 2 + zh, p,
             )
         send(
-            wb.at[partner, w_rows(ch), :], wb.at[partner, w_rows(ch), :], ssem.at[10],
+            wb.at[w_rows(partner, ch), :], wb.at[w_rows(partner, ch), :], ssem.at[10],
             rww, s, sib,
         )
 
     def w_sibling(ch, far):
         for d in (1, 3, 2):
             shard = ((x + d) % 4) * 2 + (partner % 2 if far else zh)
-            wait(wb.at[shard, w_rows(ch), :], rwx.at[ch, (4 if far else 0) + d])
+            wait(wb.at[w_rows(shard, ch), :], rwx.at[ch, (4 if far else 0) + d])
             send(
-                wb.at[shard, w_rows(ch), :], wb.at[shard, w_rows(ch), :], ssem.at[10],
+                wb.at[w_rows(shard, ch), :], wb.at[w_rows(shard, ch), :], ssem.at[10],
                 rww, s, sib,
             )
 
@@ -123,6 +128,26 @@
     w_over(0)
 
     part[:, 6:8, :] = jnp.zeros((64, 2, 128), F32)
+
+    def v_unit(block, unit, way, step, target):
+        send(
+            vg.at[c, block, unit], vg.at[c, block, unit], ssem.at[13], rvr.at[way, step, unit], s, target
+        )
+
+    def v_sib(block):
+        send(vg.at[c, block], vg.at[c, block], ssem.at[14], rvs, s, sib)
+
+    def v_step(step):
+        below, above = (y + 8 - step) % 8, (y + step) % 8
+        for unit in range(4):
+            wait(vg.at[0, 0, 0], rvr.at[0, step - 1, unit])
+            if step < 3 or unit < 2:
+                v_unit(below, unit, 0, step, up)
+            wait(vg.at[0, 0, 0], rvr.at[1, step - 1, unit])
+            if step < 3 or unit >= 2:
+                v_unit(above, unit, 1, step, down)
+        v_sib(below)
+        v_sib(above)
 
     for d in (1, 3, 2):
         other = (zl + d) % 4
@@ -134,6 +159,13 @@
     loads[1].wait()
     for other in range(4):
         wait(qg.at[0], rqs.at[other])
+    loads[2].wait()
+    for d in (1, 3, 2):
+        other = (zl + d) % 4
+        wait(vg.at[0, 0, 0], rva.at[other])
+        v_unit(y, other, 0, 0, up)
+        v_unit(y, other, 1, 0, down)
+    v_sib(y)
     wait(kg.at[0:7], rk)
 
     lane64 = lax.broadcasted_iota(jnp.int32, (64, 128), 1) < 64
@@ -151,46 +183,15 @@
     own = pltpu.make_async_copy(part.at[zc * 8 + s], rs.at[plane], lsem.at[7])
     own.start()
 
-    def scatter(d, carry):
-        o = (plane + d) % 64
-        so, zo = o // 8, o % 8
+    for d in range(1, 64):
+        so, zo = (s + d // 8) % 8, (zc + d % 8) % 8
         send(part.at[zo * 8 + so], rs.at[plane], ssem.at[11], rrs, so, y * 8 + zo)
-        return carry
-
-    lax.fori_loop(1, 64, scatter, 0)
-
-    up, down = ((y + 1) % 8) * 8 + zc, ((y + 7) % 8) * 8 + zc
-
-    def v_send(block, step, halves):
-        if halves:
-            send(
-                vg.at[c, block[0], 0:2], vg.at[c, block[0], 0:2], ssem.at[12], rvr.at[0, step], s, up
-            )
-            send(
-                vg.at[c, block[1], 2:4], vg.at[c, block[1], 2:4], ssem.at[12], rvr.at[1, step], s, down
-            )
-            return
-        send(vg.at[c, block[0]], vg.at[c, block[0]], ssem.at[13], rvr.at[0, step], s, up)
-        send(vg.at[c, block[1]], vg.at[c, block[1]], ssem.at[13], rvr.at[1, step], s, down)
-
-    def v_sib(block):
-        send(vg.at[c, block], vg.at[c, block], ssem.at[14], rvs, s, sib)
-
-    loads[2].wait()
-    wait(vg.at[0, 0, 0:3], rva)
-    v_send((y, y), 0, False)
-    v_sib(y)
-
-    def v_step(step):
-        below, above = (y + 8 - step) % 8, (y + step) % 8
-        wait(vg.at[0, 0], rvr.at[0, step - 1])
-        wait(vg.at[0, 0], rvr.at[1, step - 1])
-        v_send((below, above), step, step == 3)
-        v_sib(below)
-        v_sib(above)
-
+
+    for ch in range(1, CHUNKS):
+        w_over(ch)
     v_step(1)
-
+    w_relay(0)
+    v_step(2)
     own.wait()
     wait(rs.at[0:63], rrs)
     logits = rs[0:8]
@@ -219,12 +220,11 @@
     keep.start()
     for d in seq_order:
         send(wm, wg.at[s], ssem.at[15], rwg, (s + d) % 8, p)
+    v_step(3)
     for ch in range(1, CHUNKS):
-        w_over(ch)
-
-    for step in (2, 3):
-        v_step(step)
-    w_relay(0)
+        w_relay(ch)
+    for ch in range(CHUNKS):
+        w_sibling(ch, False)
 
     keep.wait()
     wait(wg.at[0:7], rwg)
@@ -248,6 +248,7 @@
     for d in range(1, 8):
         send(ptl.at[s], ptz.at[zc], ssem.at[16], rpz, s, y * 8 + (zc + d) % 8)
 
+    loads[8].wait()
     for z in range(4):
         acc = zero8
         for k in range(6):
@@ -260,9 +261,8 @@
         for d in y_order:
             send(mloc, mrow, ssem.at[17], rm1, s, ((y + d) % 8) * 8 + zc)
 
-    for step in (3,):
-        wait(vg.at[0, 0, 0:2], rvr.at[0, step])
-        wait(vg.at[0, 0, 2:4], rvr.at[1, step])
+    for unit in range(4):
+        wait(vg.at[0, 0, 0], rvr.at[unit // 2, 3, unit])
     opposite = (y + 4) % 8
     v_sib(opposite)
     wait(vg.at[0], rvs)
@@ -297,6 +297,7 @@
     ).astype(BF16)
     loads[4].wait()
     loads[6].wait()
+    loads[7].wait()
     skip = jnp.concatenate(
         [
             jnp.concatenate([sk[r, k].astype(F32) for k in range(6)], axis=1)
@@ -304,12 +305,13 @@
         ],
         axis=0,
     )
+    scaling = jnp.concatenate([gain[k : k + 1, :] for k in range(6)], axis=1)
     hidden = skip + jnp.dot(row_out, wc[...], preferred_element_type=F32)
     hid[...] = hidden
     average = jnp.mean(hidden, axis=1, keepdims=True)
     centered = hidden - average
     spread = jnp.mean(centered * centered, axis=1, keepdims=True)
-    normed = centered * lax.rsqrt(spread + 1e-05) * gain_ref[...]
+    normed = centered * lax.rsqrt(spread + 1e-05) * scaling
     for r in range(4):
         for k in range(6):
             nf[:, r * 6 + k, :] = normed[r * 8 : r * 8 + 8, k * 128 : k * 128 + 128]
@@ -318,11 +320,6 @@
     keep.start()
     for d in seq_order:
         send(nm.at[(s + d) % 8], ng.at[s], ssem.at[18], rng, (s + d) % 8, p)
-
-    for ch in range(1, CHUNKS):
-        w_relay(ch)
-    for ch in range(CHUNKS):
-        w_sibling(ch, False)
 
     wait(ptz.at[0:7], rpz)
     acc = ptz[0]
@@ -335,7 +332,29 @@
     for ch in range(CHUNKS):
         w_sibling(ch, True)
     loads[3].wait()
-    wait(wb.at[0:7, 0:384, :], rww)
+    wait(wb.at[0:1008, :], rww)
+
+    wait(pty.at[0:7], rpy)
+    acc = pty[0]
+    for o in range(1, 8):
+        acc = acc + pty[o]
+    stage[1] = acc
+    pts[s] = acc
+    for d in seq_order:
+        send(stage.at[1], pts.at[s], ssem.at[21], rps, (s + d) % 8, p)
+
+    @pl.when(y == s)
+    def _():
+        mrow[...] = mloc[...]
+
+    @pl.when(y != s)
+    def _():
+        wait(mrow, rm1)
+
+    mcol[zc] = mrow[zl]
+    for d in range(1, 8):
+        o = (zc + d) % 8
+        send(mrow.at[o // 2], mcol.at[zc], ssem.at[22], rm2, s, y * 8 + o)
 
     def unpack(ref):
         nf[...] = ref[...].astype(F32)
@@ -350,17 +369,14 @@
     keep.wait()
     wait(ng.at[0:7], rng)
     cells = unpack(ng)
-    for so in range(8):
-        proj[:, so * 288 : so * 288 + 288] = jnp.dot(
-            cells, wb[so], preferred_element_type=F32
-        )
+    proj[...] = lax.dot_general(cells, wb[...], NT, preferred_element_type=F32).astype(BF16)
     lane32 = lax.broadcasted_iota(jnp.int32, (32, 128), 1) < 64
     zero32 = jnp.zeros((32, 128), BF16)
     outs = []
     for k in range(6):
-        cq = proj[:, k * 128 : k * 128 + 128].astype(BF16)
-        ck = proj[:, 768 + k * 128 : 768 + k * 128 + 128].astype(BF16)
-        cv = proj[:, 1536 + k * 128 : 1536 + k * 128 + 128].astype(BF16)
+        cq = proj[:, k * 128 : k * 128 + 128]
+        ck = proj[:, 768 + k * 128 : 768 + k * 128 + 128]
+        cv = proj[:, 1536 + k * 128 : 1536 + k * 128 + 128]
         left = jnp.concatenate(
             [jnp.where(lane32, cq, zero32), jnp.where(lane32, zero32, cq)], axis=0
         )
@@ -377,37 +393,6 @@
     keep.start()
     for d in seq_order:
         send(cm.at[(s + d) % 8], cg.at[s], ssem.at[20], rcg, (s + d) % 8, p)
-
-    wait(pty.at[0:7], rpy)
-    acc = pty[0]
-    for o in range(1, 8):
-        acc = acc + pty[o]
-    stage[1] = acc
-    pts[s] = acc
-    for d in seq_order:
-        send(stage.at[1], pts.at[s], ssem.at[21], rps, (s + d) % 8, p)
-
-    @pl.when(y == s)
-    def _():
-        mrow[...] = mloc[...]
-
-    @pl.when(y != s)
-    def _():
-        wait(mrow, rm1)
-
-    mcol[zc] = mrow[zl]
-    for d in range(1, 8):
-        o = (zc + d) % 8
-        send(mrow.at[o // 2], mcol.at[zc], ssem.at[22], rm2, s, y * 8 + o)
-
-    loads[5].wait()
-    keep.wait()
-    wait(cg.at[0:7], rcg)
-    cells = unpack(cg)
-    closing = hid[...] + jnp.dot(cells, wo[...], preferred_element_type=F32)
-    for r in range(4):
-        for k in range(6):
-            out_ref[r, k] = closing[r * 8 : r * 8 + 8, k * 128 : k * 128 + 128].astype(BF16)
 
     wait(pts.at[0:7], rps)
     wait(mcol.at[0:7], rm2)
@@ -440,18 +425,26 @@
     )
     pair_ref[...] = jax.nn.sigmoid(block[16:24] + mirrored - product + offset_ref[0])
 
+    loads[5].wait()
+    keep.wait()
+    wait(cg.at[0:7], rcg)
+    cells = unpack(cg)
+    closing = hid[...] + jnp.dot(cells, wo[...], preferred_element_type=F32)
+    for r in range(4):
+        for k in range(6):
+            out_ref[r, k] = closing[r * 8 : r * 8 + 8, k * 128 : k * 128 + 128].astype(BF16)
+
     wait(qg.at[0:4], ssem.at[0])
     wait(qg.at[0:3], ssem.at[1])
     wait(kg.at[0:7], ssem.at[2])
     wait(vg.at[0, 0, 0:3], ssem.at[3])
     for ch in range(CHUNKS):
-        wait(wb.at[0:3, 0:rows, :], ssem.at[4 + ch])
-        wait(wb.at[0, 0:rows, :], ssem.at[6 + ch])
-        wait(wb.at[0:3, 0:rows, :], ssem.at[8 + ch])
-    wait(wb.at[0:7, 0:384, :], ssem.at[10])
+        wait(wb.at[0 : 3 * W_ROWS[ch], :], ssem.at[4 + ch])
+        wait(wb.at[0 : W_ROWS[ch], :], ssem.at[6 + ch])
+        wait(wb.at[0 : 3 * W_ROWS[ch], :], ssem.at[8 + ch])
+    wait(wb.at[0:1008, :], ssem.at[10])
     wait(rs.at[0:63], ssem.at[11])
-    wait(vg.at[0, 0], ssem.at[12])
-    wait(vg.at[0, 0:6], ssem.at[13])
+    wait(vg.at[0, 0:7], ssem.at[13])
     wait(vg.at[0], ssem.at[14])
     wait(wg.at[0:7], ssem.at[15])
     wait(ptz.at[0:7], ssem.at[16])
@@ -488,9 +481,8 @@
     def dma(*shape):
         return pltpu.SemaphoreType.DMA(shape)
 
-    anywhere = pl.BlockSpec(memory_space=pl.ANY)
+    anywhere = pl.BlockSpec(memory_space=pltpu.HBM)
     in_vmem = pl.BlockSpec(memory_space=pltpu.VMEM)
-    in_smem = pl.BlockSpec(memory_space=pltpu.SMEM)
     one = pltpu.SemaphoreType.DMA
     aligned, pairs = pl.pallas_call(
         body,
@@ -498,16 +490,13 @@
             jax.ShapeDtypeStruct((4, 6, 8, 128), BF16),
             jax.ShapeDtypeStruct((8, 64), F32),
         ),
-        in_specs=[
-            anywhere, anywhere, anywhere, anywhere, anywhere, in_vmem, anywhere, anywhere,
-            in_smem, in_smem,
-        ],
+        in_specs=[anywhere] * 9 + [pl.BlockSpec(memory_space=pltpu.SMEM)],
         out_specs=(in_vmem, in_vmem),
         scratch_shapes=[
             vmem(8, 4, 6, 8, 128),
             vmem(8, 4, 6, 8, 128),
             vmem(2, 8, 4, 4, 6, 8, 128),
-            vmem(8, 768, 288),
+            vmem(2304, 768),
             vmem(768, 768),
             vmem(768, 768),
             vmem(4, 6, 8, 128),
@@ -522,7 +511,9 @@
             vmem(8, 24, 128),
             vmem(8, 24, 128),
             vmem(32, 768, dtype=F32),
-            vmem(32, 2304, dtype=F32),
+            vmem(32, 2304),
+            vmem(6, 128, dtype=F32),
+            pltpu.SMEM((12,), F32),
             vmem(8, 8, 128, dtype=F32),
             vmem(8, 8, 128, dtype=F32),
             vmem(8, 8, 128, dtype=F32),
@@ -531,14 +522,14 @@
             vmem(4, 8, 128, dtype=F32),
             vmem(8, 8, 128, dtype=F32),
             vmem(2, 8, 128, dtype=F32),
-            dma(11),
+            dma(14),
             dma(23),
             dma(4),
             dma(4),
             one,
-            one,
-            one,
-            dma(2, 4),
+            dma(4),
+            one,
+            dma(2, 4, 4),
             dma(CHUNKS, 8),
             one,
             one,
@@ -552,7 +543,7 @@
             one,
         ],
         compiler_params=pltpu.CompilerParams(
-            collective_id=0, has_side_effects=True, vmem_limit_bytes=48 << 20
+            collective_id=0, has_side_effects=True, vmem_limit_bytes=62 << 20
         ),
         name="axial_layer",
     )(
@@ -561,8 +552,8 @@
         tiles(lateral_matched_vectors),
         tiles(lateral_carried_vectors),
         lateral_closing_linear,
-        upright_normalizer_multiplier.reshape(1, 768),
-        upright_threefold_linear,
+        upright_normalizer_multiplier.reshape(6, 128),
+        upright_threefold_linear.T,
         upright_closing_linear,
         regression_factors,
         regression_offset,

time: 93 us -> 74.4 us (0.80)
  Pallas kernels: 81.5 us -> 70.2 us
  local copies, waits for them, and re-layouts: 9.6 us -> 2.69 us
    pallas_call x1, Pallas kernels: 81.5 us -> 70.2 us  [per_device(): pl.pallas_call(body, out_shape=(jax.ShapeDtypeStruct((4, 6, 8, 128), BF16...]
    unnamed x17 -> x2, local copies, waits for them, and re-layouts: 8.91 us -> 2.69 us
where the time goes in v2:
time: 74.4 us; the launch traced here: 74.2 us
  Pallas kernels  70.2 us (94%)
  local copies, waits for them, and re-layouts  2.69 us (4%)
  between operations  1.29 us (2%)
    pallas_call x1, Pallas kernels, per_device(): pl.pallas_call(body, out_shape=(jax.ShapeDtypeStruct((4, 6, 8, 128), BF16...  70.2 us
    unnamed x2, local copies, waits for them, and re-layouts  2.69 us

profile of v2, /device:TPU:1, one launch (start us, length us, event | category | flops | bytes accessed | tf_op | source)
XLA Modules:
  0.0 74.2 jit_solution(1391559646531071299)
XLA Ops:
  1.3 70.2 %axial_layer.1 = (bf16[4,6,8,128]{3,2,1,0:T(8,128)(2,1)}, f32[8,64]{1,0:T(8,128)}) custom-call(bf16[4,6,8,128]{3,2,1,0:T(8,128)(2,1)} %bitcast.19, bf16[4,6,8,128]{3,2,1,0:T(8,128)(2,1)} %bitcast.20, bf16[4,6,8,128]{3,2,1,0:T(8,128)(2,1)} %bitcast.21, bf16[4,6,8,128]{3,2,1,0:T(8,128)(2,1)} %bitcast.22, bf16[768,768]{1,0:T(8,128)(2,1)} %wc_hbm.1, ...), custom_call_target="tpu_custom_call" | custom-call | tf_op jit(solution)/shard_map/axial_layer/pallas_call | solution.py:487
  71.5 1.4 %copy.15 = bf16[4,8,768]{2,1,0:T(8,128)(2,1)} copy(bf16[4,8,768]{2,1,0:T(8,128)(2,1)} %bitcast.18) | data formatting | bytes 98304
  73.0 1.3 %copy.16 = f32[8,64]{1,0:T(8,128)} copy(f32[8,64]{1,0:T(8,128)} %get-tuple-element.9) | data formatting | bytes 4096

commit v3 on v2

--- a/solution.py
+++ b/solution.py
@@ -12,17 +12,15 @@
 F32 = jnp.float32
 BF16 = jnp.bfloat16
 NT = (((1,), (1,)), ((), ()))
-CHUNKS = 2
-W_AT, W_ROWS = (0, 80), (80, 64)
 
 
 def body(
     skip_hbm, q_hbm, k_hbm, v_hbm, wc_hbm, gain_hbm, w3_hbm, wo_hbm, factor_hbm, offset_ref,
     out_ref, pair_ref,
     qg, kg, vg, wb, wc, wo, sk,
-    part, rs, wm, wg, wf, nf, nm, ng, cm, cg, hid, proj, gain, factor_ref,
+    part, rs, wm, wg, wf, nf, nm, ng, cm, cg, gf, cf, hid, proj, gain, factor_ref,
     ptl, ptz, pty, pts, mloc, mrow, mcol, stage,
-    lsem, ssem, rq, rqs, rk, rva, rvs, rvr, rwx, rww, rrs, rwg, rng, rcg, rpz, rpy, rps, rm1, rm2,
+    lsem, ssem, rq, rqs, rk, rva, rvs, rvr, rw, rww, wlocal, wsu, wsf, wss, rrs, rwg, rng, rcg, rpz, rpy, rps, rm1, rm2,
 ):
     s = lax.axis_index("seq")
     p = lax.axis_index("pos")
@@ -30,7 +28,6 @@
     y, zc = p // 8, p % 8
     zl, c = zc // 2, zc % 2
     sib = y * 8 + zl * 2 + (1 - c)
-    partner = x * 2 + (1 - zh)
 
     def local(src, dst, index):
         copy = pltpu.make_async_copy(src, dst, lsem.at[index])
@@ -46,88 +43,95 @@
     def wait(ref, sem):
         pltpu.make_async_copy(ref, ref, sem).wait()
 
+    barrier = pltpu.get_barrier_semaphore()
+    plane = s * 8 + zc
+    for d in (4, 3, 5, 2, 6, 1, 7):
+        for peer in (((s + d) % 8, p), (s, ((y + d) % 8) * 8 + zc), (s, y * 8 + (zc + d) % 8)):
+            pl.semaphore_signal(barrier, inc=1, device_id=peer, device_id_type=MESH)
     loads = [
         local(q_hbm, qg.at[zc], 0),
         local(k_hbm, kg.at[y], 1),
         local(v_hbm, vg.at[c, y, zl], 2),
-        local(w3_hbm, wb.at[pl.ds(pl.multiple_of(s * 288, 16), 288), :], 3),
+        None,
         local(wc_hbm, wc, 4),
         local(wo_hbm, wo, 5),
         local(skip_hbm, sk, 6),
         local(gain_hbm, gain, 11),
         local(factor_hbm, factor_ref, 12),
     ]
-
-    barrier = pltpu.get_barrier_semaphore()
-    plane = s * 8 + zc
-
-    for d in range(1, 64):
-        pl.semaphore_signal(
-            barrier, inc=1, device_id=((s + d // 8) % 8, y * 8 + (zc + d % 8) % 8), device_id_type=MESH
-        )
-    for d in range(1, 8):
-        pl.semaphore_signal(
-            barrier, inc=1, device_id=(s, ((y + d) % 8) * 8 + zc), device_id_type=MESH
-        )
-    pl.semaphore_wait(barrier, 70)
+    pl.semaphore_wait(barrier, 21)
 
     y_order = (4, 3, 5, 2, 6, 1, 7)
+    up, down = ((y + 1) % 8) * 8 + zc, ((y + 7) % 8) * 8 + zc
+    z_order = (2, 1, 3)
+    for d in z_order:
+        send(q_hbm, qg.at[zc], ssem.at[1], rq.at[zl], s, y * 8 + ((zl + d) % 4) * 2 + c)
     send(q_hbm, qg.at[zc], ssem.at[0], rqs.at[zl], s, sib)
-    for d in (1, 3, 2):
-        send(q_hbm, qg.at[zc], ssem.at[1], rq.at[zl], s, y * 8 + ((zl + d) % 4) * 2 + c)
+    for d in z_order:
+        send(v_hbm, vg.at[c, y, zl], ssem.at[3], rva.at[zl], s, y * 8 + ((zl + d) % 4) * 2 + c)
     for d in y_order:
         send(k_hbm, kg.at[y], ssem.at[2], rk, s, ((y + d) % 8) * 8 + zc)
-    up, down = ((y + 1) % 8) * 8 + zc, ((y + 7) % 8) * 8 + zc
-    for d in (1, 3, 2):
-        send(v_hbm, vg.at[c, y, zl], ssem.at[3], rva.at[zl], s, y * 8 + ((zl + d) % 4) * 2 + c)
     send(v_hbm, vg.at[c, y, zl], ssem.at[13], rvr.at[0, 0, zl], s, up)
     send(v_hbm, vg.at[c, y, zl], ssem.at[13], rvr.at[1, 0, zl], s, down)
 
-    def w_rows(shard, ch):
-        return pl.ds(pl.multiple_of(shard * 288 + c * 144 + W_AT[ch], 16), W_ROWS[ch])
-
-    def w_src(ch):
-        return w3_hbm.at[pl.ds(pl.multiple_of(c * 144 + W_AT[ch], 16), W_ROWS[ch]), :]
-
-    def w_own(ch):
-        for d in (1, 3, 2):
-            send(
-                w_src(ch), wb.at[w_rows(s, ch), :], ssem.at[4 + ch],
-                rwx.at[ch, (4 - d) % 4], ((x + d) % 4) * 2 + zh, p,
-            )
-
-    def w_over(ch):
-        send(
-            w_src(ch), wb.at[w_rows(s, ch), :], ssem.at[6 + ch],
-            rwx.at[ch, 4], partner, p,
-        )
-
-    def w_relay(ch):
-        wait(wb.at[w_rows(partner, ch), :], rwx.at[ch, 4])
-        for d in (1, 3, 2):
-            send(
-                wb.at[w_rows(partner, ch), :], wb.at[w_rows(partner, ch), :], ssem.at[8 + ch],
-                rwx.at[ch, 4 + (4 - d) % 4], ((x + d) % 4) * 2 + zh, p,
-            )
-        send(
-            wb.at[w_rows(partner, ch), :], wb.at[w_rows(partner, ch), :], ssem.at[10],
-            rww, s, sib,
-        )
-
-    def w_sibling(ch, far):
-        for d in (1, 3, 2):
-            shard = ((x + d) % 4) * 2 + (partner % 2 if far else zh)
-            wait(wb.at[w_rows(shard, ch), :], rwx.at[ch, (4 if far else 0) + d])
-            send(
-                wb.at[w_rows(shard, ch), :], wb.at[w_rows(shard, ch), :], ssem.at[10],
-                rww, s, sib,
-            )
-
-    for ch in range(CHUNKS):
-        w_own(ch)
-    w_over(0)
-
-    part[:, 6:8, :] = jnp.zeros((64, 2, 128), F32)
+    def x_peers(src, dst, send_sem, recv_sem):
+        for d in (2, 1, 3):
+            send(src, dst, send_sem, recv_sem, ((x + d) % 4) * 2 + zh, p)
+
+    def w_unit(u):
+        col = s * 288 + 32 * u
+        role, within = col // 768, col % 768
+        pair = within // 128
+        index = role * 12 + (pair // 2) * 4 + (within % 128) // 32
+        src = w3_hbm.at[pl.ds(pl.multiple_of(32 * u + c * 16, 16), 16), :]
+        dst = wb.at[pl.ds(pl.multiple_of(index * 32 + c * 16, 16), 16), :]
+        return pair % 2, index, src, dst
+
+    def w_near(u):
+        group, index, src, dst = w_unit(u)
+
+        @pl.when(group == zh)
+        def _():
+            pltpu.make_async_copy(src, dst, wlocal.at[u]).start()
+            x_peers(src, dst, wsu.at[u], rw.at[index])
+            send(src, dst, wsu.at[u], rww, s, sib)
+
+    def w_far(u):
+        group, index, src, dst = w_unit(u)
+
+        @pl.when(group != zh)
+        def _():
+            send(src, dst, wsu.at[u], rw.at[index], x * 2 + 1 - zh, p)
+
+    def w_place(n):
+        col = (n // 12) * 768 + (n % 12 // 4) * 256 + zh * 128 + (n % 4) * 32
+        owner = col // 288
+        here = owner // 2 == x
+        far = owner % 2 != zh
+        return far & here, jnp.logical_not(far) & here, wb.at[pl.ds(pl.multiple_of(n * 32 + c * 16, 16), 16), :]
+
+    def w_pass(n):
+        lands, mine, dst = w_place(n)
+
+        @pl.when(lands)
+        def _():
+            wait(dst, rw.at[n])
+            x_peers(dst, dst, wsf.at[n], rw.at[n])
+            send(dst, dst, wss.at[n], rww, s, sib)
+
+    def w_last(n):
+        lands, mine, dst = w_place(n)
+
+        @pl.when(jnp.logical_not(lands | mine))
+        def _():
+            wait(dst, rw.at[n])
+            send(dst, dst, wss.at[n], rww, s, sib)
+
+    for u in range(9):
+        w_near(u)
+
+    rs[:, 6:8, :] = jnp.zeros((64, 2, 128), F32)
+    wg[:, :, 6:8, :] = jnp.zeros((8, 8, 2, 128), BF16)
 
     def v_unit(block, unit, way, step, target):
         send(
@@ -137,17 +141,21 @@
     def v_sib(block):
         send(vg.at[c, block], vg.at[c, block], ssem.at[14], rvs, s, sib)
 
-    def v_step(step):
+    v_order = (0, 1, 3, 2)
+
+    def v_step(step, places):
         below, above = (y + 8 - step) % 8, (y + step) % 8
-        for unit in range(4):
+        for at in places:
+            unit = (zl + v_order[at]) % 4
             wait(vg.at[0, 0, 0], rvr.at[0, step - 1, unit])
-            if step < 3 or unit < 2:
+            if step < 3 or at < 2:
                 v_unit(below, unit, 0, step, up)
             wait(vg.at[0, 0, 0], rvr.at[1, step - 1, unit])
-            if step < 3 or unit >= 2:
+            if step < 3 or at >= 2:
                 v_unit(above, unit, 1, step, down)
-        v_sib(below)
-        v_sib(above)
+        if 3 in places:
+            v_sib(below)
+            v_sib(above)
 
     for d in (1, 3, 2):
         other = (zl + d) % 4
@@ -159,13 +167,8 @@
     loads[1].wait()
     for other in range(4):
         wait(qg.at[0], rqs.at[other])
-    loads[2].wait()
-    for d in (1, 3, 2):
-        other = (zl + d) % 4
-        wait(vg.at[0, 0, 0], rva.at[other])
-        v_unit(y, other, 0, 0, up)
-        v_unit(y, other, 1, 0, down)
-    v_sib(y)
+    for u in range(9):
+        w_far(u)
     wait(kg.at[0:7], rk)
 
     lane64 = lax.broadcasted_iota(jnp.int32, (64, 128), 1) < 64
@@ -180,20 +183,26 @@
         )
         part[:, k, :] = tile
 
-    own = pltpu.make_async_copy(part.at[zc * 8 + s], rs.at[plane], lsem.at[7])
+    own = pltpu.make_async_copy(part.at[zc * 8 + s, 0:6], rs.at[plane, 0:6], lsem.at[7])
     own.start()
 
     for d in range(1, 64):
         so, zo = (s + d // 8) % 8, (zc + d % 8) % 8
-        send(part.at[zo * 8 + so], rs.at[plane], ssem.at[11], rrs, so, y * 8 + zo)
-
-    for ch in range(1, CHUNKS):
-        w_over(ch)
-    v_step(1)
-    w_relay(0)
-    v_step(2)
+        send(part.at[zo * 8 + so, 0:6], rs.at[plane, 0:6], ssem.at[11], rrs, so, y * 8 + zo)
+
+    loads[2].wait()
+    for d in (1, 3, 2):
+        other = (zl + d) % 4
+        wait(vg.at[0, 0, 0], rva.at[other])
+        v_unit(y, other, 0, 0, up)
+        v_unit(y, other, 1, 0, down)
+    v_sib(y)
+    v_step(1, (0, 1, 2, 3))
+    for n in range(36):
+        w_pass(n)
+    v_step(2, (0, 1, 2, 3))
     own.wait()
-    wait(rs.at[0:63], rrs)
+    wait(rs.at[0:63, 0:6], rrs)
     logits = rs[0:8]
     for so in range(1, 8):
         logits = logits + rs[so * 8 : so * 8 + 8]
@@ -216,18 +225,15 @@
         wm[4 + z] = jnp.where(lower, pltpu.roll(even, 64, 1), odd).astype(BF16)
 
     seq_order = (7, 1, 2, 6, 3, 5, 4)
-    keep = pltpu.make_async_copy(wm, wg.at[s], lsem.at[8])
+    keep = pltpu.make_async_copy(wm.at[:, 0:6], wg.at[s, :, 0:6], lsem.at[8])
     keep.start()
     for d in seq_order:
-        send(wm, wg.at[s], ssem.at[15], rwg, (s + d) % 8, p)
-    v_step(3)
-    for ch in range(1, CHUNKS):
-        w_relay(ch)
-    for ch in range(CHUNKS):
-        w_sibling(ch, False)
-
+        send(wm.at[:, 0:6], wg.at[s, :, 0:6], ssem.at[15], rwg, (s + d) % 8, p)
+    v_step(3, (0, 1, 2, 3))
+    for n in range(36):
+        w_last(n)
     keep.wait()
-    wait(wg.at[0:7], rwg)
+    wait(wg.at[0:7, :, 0:6], rwg)
     wf[...] = wg[...].astype(F32)
 
     sums = wf[0]
@@ -261,8 +267,8 @@
         for d in y_order:
             send(mloc, mrow, ssem.at[17], rm1, s, ((y + d) % 8) * 8 + zc)
 
-    for unit in range(4):
-        wait(vg.at[0, 0, 0], rvr.at[unit // 2, 3, unit])
+    for at in range(4):
+        wait(vg.at[0, 0, 0], rvr.at[at // 2, 3, (zl + v_order[at]) % 4])
     opposite = (y + 4) % 8
     v_sib(opposite)
     wait(vg.at[0], rvs)
@@ -315,11 +321,12 @@
     for r in range(4):
         for k in range(6):
             nf[:, r * 6 + k, :] = normed[r * 8 : r * 8 + 8, k * 128 : k * 128 + 128]
-    nm[...] = nf[...].astype(BF16)
-    keep = pltpu.make_async_copy(nm.at[s], ng.at[s], lsem.at[9])
+    nm[:, 0] = nf[0:4].astype(BF16)
+    nm[:, 1] = nf[4:8].astype(BF16)
+    keep = pltpu.make_async_copy(nm.at[x], ng.at[s], lsem.at[9])
     keep.start()
     for d in seq_order:
-        send(nm.at[(s + d) % 8], ng.at[s], ssem.at[18], rng, (s + d) % 8, p)
+        send(nm.at[((s + d) % 8) // 2], ng.at[s], ssem.at[18], rng, (s + d) % 8, p)
 
     wait(ptz.at[0:7], rpz)
     acc = ptz[0]
@@ -329,10 +336,14 @@
     pty[y] = acc
     for d in y_order:
         send(stage.at[0], pty.at[y], ssem.at[19], rpy, s, ((y + d) % 8) * 8 + zc)
-    for ch in range(CHUNKS):
-        w_sibling(ch, True)
-    loads[3].wait()
-    wait(wb.at[0:1008, :], rww)
+    for u in range(9):
+        group, index, src, dst = w_unit(u)
+
+        @pl.when(group == zh)
+        def _():
+            pltpu.make_async_copy(src, dst, wlocal.at[u]).wait()
+
+    wait(wb.at[0:576, :], rww)
 
     wait(pty.at[0:7], rpy)
     acc = pty[0]
@@ -356,43 +367,43 @@
         o = (zc + d) % 8
         send(mrow.at[o // 2], mcol.at[zc], ssem.at[22], rm2, s, y * 8 + o)
 
-    def unpack(ref):
-        nf[...] = ref[...].astype(F32)
-        return jnp.concatenate(
-            [
-                jnp.concatenate([nf[:, r * 6 + k, :] for k in range(6)], axis=1)
-                for r in range(4)
-            ],
-            axis=0,
-        ).astype(BF16)
-
     keep.wait()
     wait(ng.at[0:7], rng)
-    cells = unpack(ng)
+    gf[...] = ng[...].astype(F32)
+    cells = jnp.concatenate(
+        [
+            jnp.concatenate([gf[:, b, r * 6 + k, :] for k in range(6)], axis=1)
+            for r in range(4)
+            for b in range(2)
+        ],
+        axis=0,
+    ).astype(BF16)
     proj[...] = lax.dot_general(cells, wb[...], NT, preferred_element_type=F32).astype(BF16)
-    lane32 = lax.broadcasted_iota(jnp.int32, (32, 128), 1) < 64
-    zero32 = jnp.zeros((32, 128), BF16)
-    outs = []
-    for k in range(6):
+    lane_low = lax.broadcasted_iota(jnp.int32, (64, 128), 1) < 64
+    same = (
+        lax.broadcasted_iota(jnp.int32, (128, 64), 0) // 8 % 2
+        == lax.broadcasted_iota(jnp.int32, (128, 64), 1) // 8 % 2
+    )
+    for k in range(3):
         cq = proj[:, k * 128 : k * 128 + 128]
-        ck = proj[:, 768 + k * 128 : 768 + k * 128 + 128]
-        cv = proj[:, 1536 + k * 128 : 1536 + k * 128 + 128]
+        ck = proj[:, 384 + k * 128 : 384 + k * 128 + 128]
+        cv = proj[:, 768 + k * 128 : 768 + k * 128 + 128]
         left = jnp.concatenate(
-            [jnp.where(lane32, cq, zero32), jnp.where(lane32, zero32, cq)], axis=0
+            [jnp.where(lane_low, cq, zero64), jnp.where(lane_low, zero64, cq)], axis=0
         )
         score = lax.dot_general(left, ck, NT, preferred_element_type=F32) * (1.0 / math.sqrt(64))
-        exponent = jnp.exp(score)
+        exponent = jnp.where(same, jnp.exp(score), 0.0)
         share = (exponent / jnp.sum(exponent, axis=1, keepdims=True)).astype(BF16)
         both = jnp.dot(share, cv, preferred_element_type=F32)
-        outs.append(jnp.where(lane32, both[0:32], both[32:64]))
-    for r in range(4):
-        for k in range(6):
-            nf[:, r * 6 + k, :] = outs[k][r * 8 : r * 8 + 8]
+        mix = jnp.where(lane_low, both[0:64], both[64:128])
+        for r in range(4):
+            for b in range(2):
+                nf[:, b * 12 + r * 3 + k, :] = mix[r * 16 + b * 8 : r * 16 + b * 8 + 8]
     cm[...] = nf[...].astype(BF16)
-    keep = pltpu.make_async_copy(cm.at[s], cg.at[s], lsem.at[10])
+    keep = pltpu.make_async_copy(cm.at[s], cg.at[zh, x], lsem.at[10])
     keep.start()
     for d in seq_order:
-        send(cm.at[(s + d) % 8], cg.at[s], ssem.at[20], rcg, (s + d) % 8, p)
+        send(cm.at[(s + d) % 8], cg.at[zh, x], ssem.at[20], rcg, (s + d) % 8, p)
 
     wait(pts.at[0:7], rps)
     wait(mcol.at[0:7], rm2)
@@ -400,7 +411,7 @@
     scaled, cols = [], []
     for hh in range(2):
         whole = pts[hh * 4] + pts[hh * 4 + 1] + pts[hh * 4 + 2] + pts[hh * 4 + 3]
-        head_total = jnp.sum(whole, axis=1, keepdims=True)
+        head_total = jnp.where(row8 < 6, jnp.sum(whole, axis=1, keepdims=True), 1.0)
         factor = zero8
         for k in range(6):
             factor = jnp.where(row8 == k, factor_ref[2 * k + hh], factor)
@@ -427,8 +438,23 @@
 
     loads[5].wait()
     keep.wait()
-    wait(cg.at[0:7], rcg)
-    cells = unpack(cg)
+    wait(cm.at[0:7], rcg)
+    cf[...] = cg[...].astype(F32)
+    cells = jnp.concatenate(
+        [
+            jnp.concatenate(
+                [
+                    jnp.concatenate(
+                        [cf[k % 2, :, b * 12 + r * 3 + k // 2, :] for b in range(2)], axis=0
+                    )
+                    for k in range(6)
+                ],
+                axis=1,
+            )
+            for r in range(4)
+        ],
+        axis=0,
+    ).astype(BF16)
     closing = hid[...] + jnp.dot(cells, wo[...], preferred_element_type=F32)
     for r in range(4):
         for k in range(6):
@@ -438,15 +464,32 @@
     wait(qg.at[0:3], ssem.at[1])
     wait(kg.at[0:7], ssem.at[2])
     wait(vg.at[0, 0, 0:3], ssem.at[3])
-    for ch in range(CHUNKS):
-        wait(wb.at[0 : 3 * W_ROWS[ch], :], ssem.at[4 + ch])
-        wait(wb.at[0 : W_ROWS[ch], :], ssem.at[6 + ch])
-        wait(wb.at[0 : 3 * W_ROWS[ch], :], ssem.at[8 + ch])
-    wait(wb.at[0:1008, :], ssem.at[10])
-    wait(rs.at[0:63], ssem.at[11])
+    for u in range(9):
+        group = w_unit(u)[0]
+
+        @pl.when(group == zh)
+        def _():
+            wait(wb.at[0:64, :], wsu.at[u])
+
+        @pl.when(group != zh)
+        def _():
+            wait(wb.at[0:16, :], wsu.at[u])
+
+    for n in range(36):
+        lands, mine, dst = w_place(n)
+
+        @pl.when(lands)
+        def _():
+            wait(wb.at[0:48, :], wsf.at[n])
+
+        @pl.when(jnp.logical_not(mine))
+        def _():
+            wait(wb.at[0:16, :], wss.at[n])
+
+    wait(rs.at[0:63, 0:6], ssem.at[11])
     wait(vg.at[0, 0:7], ssem.at[13])
     wait(vg.at[0], ssem.at[14])
-    wait(wg.at[0:7], ssem.at[15])
+    wait(wg.at[0:7, :, 0:6], ssem.at[15])
     wait(ptz.at[0:7], ssem.at[16])
 
     @pl.when(y == s)
@@ -455,7 +498,7 @@
 
     wait(ng.at[0:7], ssem.at[18])
     wait(pty.at[0:7], ssem.at[19])
-    wait(cg.at[0:7], ssem.at[20])
+    wait(cm.at[0:7], ssem.at[20])
     wait(pts.at[0:7], ssem.at[21])
     wait(mcol.at[0:7], ssem.at[22])
 
@@ -496,7 +539,7 @@
             vmem(8, 4, 6, 8, 128),
             vmem(8, 4, 6, 8, 128),
             vmem(2, 8, 4, 4, 6, 8, 128),
-            vmem(2304, 768),
+            vmem(1152, 768),
             vmem(768, 768),
             vmem(768, 768),
             vmem(4, 6, 8, 128),
@@ -506,12 +549,14 @@
             vmem(8, 8, 8, 128),
             vmem(8, 8, 8, 128, dtype=F32),
             vmem(8, 24, 128, dtype=F32),
+            vmem(4, 2, 24, 128),
+            vmem(8, 2, 24, 128),
             vmem(8, 24, 128),
-            vmem(8, 24, 128),
-            vmem(8, 24, 128),
-            vmem(8, 24, 128),
+            vmem(2, 4, 24, 128),
+            vmem(8, 2, 24, 128, dtype=F32),
+            vmem(2, 4, 24, 128, dtype=F32),
             vmem(32, 768, dtype=F32),
-            vmem(32, 2304),
+            vmem(64, 1152),
             vmem(6, 128, dtype=F32),
             pltpu.SMEM((12,), F32),
             vmem(8, 8, 128, dtype=F32),
@@ -530,8 +575,12 @@
             dma(4),
             one,
             dma(2, 4, 4),
-            dma(CHUNKS, 8),
-            one,
+            dma(36),
+            one,
+            dma(9),
+            dma(9),
+            dma(36),
+            dma(36),
             one,
             one,
             one,

time: 74.4 us -> 67.6 us (0.909)
  Pallas kernels: 70.2 us -> 63.3 us
    pallas_call x1, Pallas kernels: 70.2 us -> 63.3 us  [per_device(): pl.pallas_call(body, out_shape=(jax.ShapeDtypeStruct((4, 6, 8, 128), BF16...]
where the time goes in v3:
time: 67.6 us; the launch traced here: 67.2 us
  Pallas kernels  63.3 us (94%)
  local copies, waits for them, and re-layouts  2.69 us (4%)
  between operations  1.29 us (2%)
    pallas_call x1, Pallas kernels, per_device(): pl.pallas_call(body, out_shape=(jax.ShapeDtypeStruct((4, 6, 8, 128), BF16...  63.3 us
    unnamed x2, local copies, waits for them, and re-layouts  2.69 us

profile of v3, /device:TPU:1, one launch (start us, length us, event | category | flops | bytes accessed | tf_op | source)
XLA Modules:
  0.0 67.2 jit_solution(7738725712797780781)
XLA Ops:
  1.3 63.3 %axial_layer.1 = (bf16[4,6,8,128]{3,2,1,0:T(8,128)(2,1)}, f32[8,64]{1,0:T(8,128)}) custom-call(bf16[4,6,8,128]{3,2,1,0:T(8,128)(2,1)} %bitcast.19, bf16[4,6,8,128]{3,2,1,0:T(8,128)(2,1)} %bitcast.20, bf16[4,6,8,128]{3,2,1,0:T(8,128)(2,1)} %bitcast.21, bf16[4,6,8,128]{3,2,1,0:T(8,128)(2,1)} %bitcast.22, bf16[768,768]{1,0:T(8,128)(2,1)} %wc_hbm.1, ...), custom_call_target="tpu_custom_call" | custom-call | tf_op jit(solution)/shard_map/axial_layer/pallas_call | solution.py:530
  64.6 1.4 %copy.15 = bf16[4,8,768]{2,1,0:T(8,128)(2,1)} copy(bf16[4,8,768]{2,1,0:T(8,128)(2,1)} %bitcast.18) | data formatting | bytes 98304
  66.0 1.3 %copy.16 = f32[8,64]{1,0:T(8,128)} copy(f32[8,64]{1,0:T(8,128)} %get-tuple-element.9) | data formatting | bytes 4096

commit v4 on v3

--- a/solution.py
+++ b/solution.py
@@ -71,8 +71,6 @@
         send(v_hbm, vg.at[c, y, zl], ssem.at[3], rva.at[zl], s, y * 8 + ((zl + d) % 4) * 2 + c)
     for d in y_order:
         send(k_hbm, kg.at[y], ssem.at[2], rk, s, ((y + d) % 8) * 8 + zc)
-    send(v_hbm, vg.at[c, y, zl], ssem.at[13], rvr.at[0, 0, zl], s, up)
-    send(v_hbm, vg.at[c, y, zl], ssem.at[13], rvr.at[1, 0, zl], s, down)
 
     def x_peers(src, dst, send_sem, recv_sem):
         for d in (2, 1, 3):
@@ -167,6 +165,8 @@
     loads[1].wait()
     for other in range(4):
         wait(qg.at[0], rqs.at[other])
+    send(v_hbm, vg.at[c, y, zl], ssem.at[13], rvr.at[0, 0, zl], s, up)
+    send(v_hbm, vg.at[c, y, zl], ssem.at[13], rvr.at[1, 0, zl], s, down)
     for u in range(9):
         w_far(u)
     wait(kg.at[0:7], rk)
@@ -198,9 +198,7 @@
         v_unit(y, other, 1, 0, down)
     v_sib(y)
     v_step(1, (0, 1, 2, 3))
-    for n in range(36):
-        w_pass(n)
-    v_step(2, (0, 1, 2, 3))
+    v_step(2, (0, 1))
     own.wait()
     wait(rs.at[0:63, 0:6], rrs)
     logits = rs[0:8]
@@ -229,9 +227,10 @@
     keep.start()
     for d in seq_order:
         send(wm.at[:, 0:6], wg.at[s, :, 0:6], ssem.at[15], rwg, (s + d) % 8, p)
+    v_step(2, (2, 3))
+    for n in range(36):
+        w_pass(n)
     v_step(3, (0, 1, 2, 3))
-    for n in range(36):
-        w_last(n)
     keep.wait()
     wait(wg.at[0:7, :, 0:6], rwg)
     wf[...] = wg[...].astype(F32)
@@ -328,6 +327,8 @@
     for d in seq_order:
         send(nm.at[((s + d) % 8) // 2], ng.at[s], ssem.at[18], rng, (s + d) % 8, p)
 
+    for n in range(36):
+        w_last(n)
     wait(ptz.at[0:7], rpz)
     acc = ptz[0]
     for z in range(1, 8):
@@ -436,6 +437,47 @@
     )
     pair_ref[...] = jax.nn.sigmoid(block[16:24] + mirrored - product + offset_ref[0])
 
+    wait(qg.at[0:4], ssem.at[0])
+    wait(qg.at[0:3], ssem.at[1])
+    wait(kg.at[0:7], ssem.at[2])
+    wait(vg.at[0, 0, 0:3], ssem.at[3])
+    for u in range(9):
+        group = w_unit(u)[0]
+
+        @pl.when(group == zh)
+        def _():
+            wait(wb.at[0:64, :], wsu.at[u])
+
+        @pl.when(group != zh)
+        def _():
+            wait(wb.at[0:16, :], wsu.at[u])
+
+    for n in range(36):
+        lands, mine, dst = w_place(n)
+
+        @pl.when(lands)
+        def _():
+            wait(wb.at[0:48, :], wsf.at[n])
+
+        @pl.when(jnp.logical_not(mine))
+        def _():
+            wait(wb.at[0:16, :], wss.at[n])
+
+    wait(rs.at[0:63, 0:6], ssem.at[11])
+    wait(vg.at[0, 0:7], ssem.at[13])
+    wait(vg.at[0], ssem.at[14])
+    wait(wg.at[0:7, :, 0:6], ssem.at[15])
+    wait(ptz.at[0:7], ssem.at[16])
+
+    @pl.when(y == s)
+    def _():
+        wait(rs.at[0:28], ssem.at[17])
+
+    wait(ng.at[0:7], ssem.at[18])
+    wait(pty.at[0:7], ssem.at[19])
+    wait(pts.at[0:7], ssem.at[21])
+    wait(mcol.at[0:7], ssem.at[22])
+
     loads[5].wait()
     keep.wait()
     wait(cm.at[0:7], rcg)
@@ -460,47 +502,7 @@
         for k in range(6):
             out_ref[r, k] = closing[r * 8 : r * 8 + 8, k * 128 : k * 128 + 128].astype(BF16)
 
-    wait(qg.at[0:4], ssem.at[0])
-    wait(qg.at[0:3], ssem.at[1])
-    wait(kg.at[0:7], ssem.at[2])
-    wait(vg.at[0, 0, 0:3], ssem.at[3])
-    for u in range(9):
-        group = w_unit(u)[0]
-
-        @pl.when(group == zh)
-        def _():
-            wait(wb.at[0:64, :], wsu.at[u])
-
-        @pl.when(group != zh)
-        def _():
-            wait(wb.at[0:16, :], wsu.at[u])
-
-    for n in range(36):
-        lands, mine, dst = w_place(n)
-
-        @pl.when(lands)
-        def _():
-            wait(wb.at[0:48, :], wsf.at[n])
-
-        @pl.when(jnp.logical_not(mine))
-        def _():
-            wait(wb.at[0:16, :], wss.at[n])
-
-    wait(rs.at[0:63, 0:6], ssem.at[11])
-    wait(vg.at[0, 0:7], ssem.at[13])
-    wait(vg.at[0], ssem.at[14])
-    wait(wg.at[0:7, :, 0:6], ssem.at[15])
-    wait(ptz.at[0:7], ssem.at[16])
-
-    @pl.when(y == s)
-    def _():
-        wait(rs.at[0:28], ssem.at[17])
-
-    wait(ng.at[0:7], ssem.at[18])
-    wait(pty.at[0:7], ssem.at[19])
     wait(cm.at[0:7], ssem.at[20])
-    wait(pts.at[0:7], ssem.at[21])
-    wait(mcol.at[0:7], ssem.at[22])
 
 
 def per_device(
@@ -530,8 +532,8 @@
     aligned, pairs = pl.pallas_call(
         body,
         out_shape=(
-            jax.ShapeDtypeStruct((4, 6, 8, 128), BF16),
-            jax.ShapeDtypeStruct((8, 64), F32),
+            pltpu.VMEM((4, 6, 8, 128), BF16),
+            pltpu.VMEM((8, 64), F32),
         ),
         in_specs=[anywhere] * 9 + [pl.BlockSpec(memory_space=pltpu.SMEM)],
         out_specs=(in_vmem, in_vmem),

time: 67.6 us -> 64.9 us (0.960)
  local copies, waits for them, and re-layouts: 2.69 us -> 1.21 us
  Pallas kernels: 63.3 us -> 62.2 us
    unnamed x2, local copies, waits for them, and re-layouts: 2.69 us -> 1.21 us
    pallas_call x1, Pallas kernels: 63.3 us -> 62.2 us  [per_device(): pl.pallas_call(body, out_shape=(pltpu.VMEM((4, 6, 8, 128), BF16), pltpu.V...]
where the time goes in v4:
time: 64.9 us; the launch traced here: 64.7 us
  Pallas kernels  62.2 us (96%)
  between operations  1.29 us (2%)
  local copies, waits for them, and re-layouts  1.21 us (2%)
    pallas_call x1, Pallas kernels, per_device(): pl.pallas_call(body, out_shape=(pltpu.VMEM((4, 6, 8, 128), BF16), pltpu.V...  62.2 us

profile of v4, /device:TPU:1, one launch (start us, length us, event | category | flops | bytes accessed | tf_op | source)
XLA Modules:
  0.0 64.7 jit_solution(2589413338400769870)
XLA Ops:
  1.3 62.2 %axial_layer.1 = (bf16[4,6,8,128]{3,2,1,0:T(8,128)(2,1)S(1)}, f32[8,64]{1,0:T(8,128)S(1)}) custom-call(bf16[4,6,8,128]{3,2,1,0:T(8,128)(2,1)} %bitcast.19, bf16[4,6,8,128]{3,2,1,0:T(8,128)(2,1)} %bitcast.20, bf16[4,6,8,128]{3,2,1,0:T(8,128)(2,1)} %bitcast.21, bf16[4,6,8,128]{3,2,1,0:T(8,128)(2,1)} %bitcast.22, bf16[768,768]{1,0:T(8,128)(2,1)} %wc_hbm.1, ...), custom_call_target="tpu_custom_call" | custom-call | tf_op jit(solution)/shard_map/axial_layer/pallas_call | solution.py:532
  63.5 0.6 copy.14
  64.1 0.6 copy.15

commit v5 on v4

--- a/solution.py
+++ b/solution.py
@@ -76,8 +76,8 @@
         for d in (2, 1, 3):
             send(src, dst, send_sem, recv_sem, ((x + d) % 4) * 2 + zh, p)
 
-    def w_unit(u):
-        col = s * 288 + 32 * u
+    def w_unit(u, shard=s):
+        col = shard * 288 + 32 * u
         role, within = col // 768, col % 768
         pair = within // 128
         index = role * 12 + (pair // 2) * 4 + (within % 128) // 32
@@ -108,14 +108,14 @@
         far = owner % 2 != zh
         return far & here, jnp.logical_not(far) & here, wb.at[pl.ds(pl.multiple_of(n * 32 + c * 16, 16), 16), :]
 
-    def w_pass(n):
-        lands, mine, dst = w_place(n)
-
-        @pl.when(lands)
-        def _():
-            wait(dst, rw.at[n])
-            x_peers(dst, dst, wsf.at[n], rw.at[n])
-            send(dst, dst, wss.at[n], rww, s, sib)
+    def w_pass(u):
+        group, index, src, dst = w_unit(u, x * 2 + 1 - zh)
+
+        @pl.when(group == zh)
+        def _():
+            wait(dst, rw.at[index])
+            x_peers(dst, dst, wsf.at[index], rw.at[index])
+            send(dst, dst, wss.at[index], rww, s, sib)
 
     def w_last(n):
         lands, mine, dst = w_place(n)
@@ -171,6 +171,13 @@
         w_far(u)
     wait(kg.at[0:7], rk)
 
+    loads[2].wait()
+    for d in (1, 3, 2):
+        other = (zl + d) % 4
+        wait(vg.at[0, 0, 0], rva.at[other])
+        v_unit(y, other, 0, 0, up)
+        v_unit(y, other, 1, 0, down)
+    v_sib(y)
     lane64 = lax.broadcasted_iota(jnp.int32, (64, 128), 1) < 64
     zero64 = jnp.zeros((64, 128), BF16)
     for k in range(6):
@@ -190,15 +197,8 @@
         so, zo = (s + d // 8) % 8, (zc + d % 8) % 8
         send(part.at[zo * 8 + so, 0:6], rs.at[plane, 0:6], ssem.at[11], rrs, so, y * 8 + zo)
 
-    loads[2].wait()
-    for d in (1, 3, 2):
-        other = (zl + d) % 4
-        wait(vg.at[0, 0, 0], rva.at[other])
-        v_unit(y, other, 0, 0, up)
-        v_unit(y, other, 1, 0, down)
-    v_sib(y)
     v_step(1, (0, 1, 2, 3))
-    v_step(2, (0, 1))
+    v_step(2, (0, 1, 2))
     own.wait()
     wait(rs.at[0:63, 0:6], rrs)
     logits = rs[0:8]
@@ -227,9 +227,9 @@
     keep.start()
     for d in seq_order:
         send(wm.at[:, 0:6], wg.at[s, :, 0:6], ssem.at[15], rwg, (s + d) % 8, p)
-    v_step(2, (2, 3))
-    for n in range(36):
-        w_pass(n)
+    v_step(2, (3,))
+    for u in range(9):
+        w_pass(u)
     v_step(3, (0, 1, 2, 3))
     keep.wait()
     wait(wg.at[0:7, :, 0:6], rwg)
@@ -266,10 +266,11 @@
         for d in y_order:
             send(mloc, mrow, ssem.at[17], rm1, s, ((y + d) % 8) * 8 + zc)
 
-    for at in range(4):
-        wait(vg.at[0, 0, 0], rvr.at[at // 2, 3, (zl + v_order[at]) % 4])
     opposite = (y + 4) % 8
-    v_sib(opposite)
+    for at in (0, 3, 1, 2):
+        unit = (zl + v_order[at]) % 4
+        wait(vg.at[0, 0, 0], rvr.at[at // 2, 3, unit])
+        send(vg.at[c, opposite, unit], vg.at[c, opposite, unit], ssem.at[14], rvs, s, sib)
     wait(vg.at[0], rvs)
 
     lower16 = lax.broadcasted_iota(jnp.int32, (8, 512), 1) % 128 < 64

time: 64.9 us -> 64.7 us (level)
  no operation moved by 1% of the time
where the time goes in v5:
time: 64.7 us; the launch traced here: 64.6 us
  Pallas kernels  62.1 us (96%)
  between operations  1.29 us (2%)
  local copies, waits for them, and re-layouts  1.21 us (2%)
    pallas_call x1, Pallas kernels, per_device(): pl.pallas_call(body, out_shape=(pltpu.VMEM((4, 6, 8, 128), BF16), pltpu.V...  62.1 us

profile of v5, /device:TPU:1, one launch (start us, length us, event | category | flops | bytes accessed | tf_op | source)
XLA Modules:
  0.0 64.6 jit_solution(9144518712392130057)
XLA Ops:
  1.3 62.1 %axial_layer.1 = (bf16[4,6,8,128]{3,2,1,0:T(8,128)(2,1)S(1)}, f32[8,64]{1,0:T(8,128)S(1)}) custom-call(bf16[4,6,8,128]{3,2,1,0:T(8,128)(2,1)} %bitcast.19, bf16[4,6,8,128]{3,2,1,0:T(8,128)(2,1)} %bitcast.20, bf16[4,6,8,128]{3,2,1,0:T(8,128)(2,1)} %bitcast.21, bf16[4,6,8,128]{3,2,1,0:T(8,128)(2,1)} %bitcast.22, bf16[768,768]{1,0:T(8,128)(2,1)} %wc_hbm.1, ...), custom_call_target="tpu_custom_call" | custom-call | tf_op jit(solution)/shard_map/axial_layer/pallas_call | solution.py:533
  63.3 0.6 copy.14
  64.0 0.6 copy.15

commit v6 on v5

--- a/solution.py
+++ b/solution.py
@@ -198,7 +198,7 @@
         send(part.at[zo * 8 + so, 0:6], rs.at[plane, 0:6], ssem.at[11], rrs, so, y * 8 + zo)
 
     v_step(1, (0, 1, 2, 3))
-    v_step(2, (0, 1, 2))
+    v_step(2, (0, 1, 2, 3))
     own.wait()
     wait(rs.at[0:63, 0:6], rrs)
     logits = rs[0:8]
@@ -227,7 +227,6 @@
     keep.start()
     for d in seq_order:
         send(wm.at[:, 0:6], wg.at[s, :, 0:6], ssem.at[15], rwg, (s + d) % 8, p)
-    v_step(2, (3,))
     for u in range(9):
         w_pass(u)
     v_step(3, (0, 1, 2, 3))

time: 64.7 us -> 64.2 us (level)
  no operation moved by 1% of the time
where the time goes in v6:
time: 64.2 us; the launch traced here: 64.1 us
  Pallas kernels  61.6 us (96%)
  between operations  1.29 us (2%)
  local copies, waits for them, and re-layouts  1.21 us (2%)
    pallas_call x1, Pallas kernels, per_device(): pl.pallas_call(body, out_shape=(pltpu.VMEM((4, 6, 8, 128), BF16), pltpu.V...  61.6 us

profile of v6, /device:TPU:1, one launch (start us, length us, event | category | flops | bytes accessed | tf_op | source)
XLA Modules:
  0.0 64.1 jit_solution(497282403322304015)
XLA Ops:
  1.3 61.6 %axial_layer.1 = (bf16[4,6,8,128]{3,2,1,0:T(8,128)(2,1)S(1)}, f32[8,64]{1,0:T(8,128)S(1)}) custom-call(bf16[4,6,8,128]{3,2,1,0:T(8,128)(2,1)} %bitcast.19, bf16[4,6,8,128]{3,2,1,0:T(8,128)(2,1)} %bitcast.20, bf16[4,6,8,128]{3,2,1,0:T(8,128)(2,1)} %bitcast.21, bf16[4,6,8,128]{3,2,1,0:T(8,128)(2,1)} %bitcast.22, bf16[768,768]{1,0:T(8,128)(2,1)} %wc_hbm.1, ...), custom_call_target="tpu_custom_call" | custom-call | tf_op jit(solution)/shard_map/axial_layer/pallas_call | solution.py:532
  62.9 0.6 copy.14
  63.5 0.6 copy.15
